TPU v7x, 32 devices: a whole 2x2x4 slice. The times are simulated.
32 devices in a mesh: dp: 16 (over z, y, x), mp: 2 (over core).
Axes of the slice: x: 2, y: 2, z: 4, core: 2. Of those that a mesh axis runs over, the one named last changes fastest.
Arguments:
- query_in: bfloat16 [32, 64, 768], P('dp'), may hold values from -6 to 6
- passage_in: bfloat16 [32, 512, 768], P('dp'), may hold values from -6 to 6
- query_len: int32 [32], P('dp'), may hold values from 8 to 64, as said below
- passage_len: int32 [32], P('dp'), may hold values from 64 to 512, as said below
- positive: int32 [32], P('dp'), may hold values from 0 to 31, each once
- step: int32 [1], replicated, may hold values from 2 to 7
- rates: float32 [5], replicated, may hold values from 0.02 to 0.6, as said below
- attn_master: float32 [4, 768, 768], P(None, 'dp', 'mp')
- attn_first: float32 [4, 768, 768], P(None, 'dp', 'mp')
- attn_second: float32 [4, 768, 768], P(None, 'dp', 'mp'), as said below
- attn_average: float32 [4, 768, 768], P(None, 'dp', 'mp')
- ffn_master: float32 [2, 768, 3072], P(None, 'dp', 'mp')
- ffn_first: float32 [2, 768, 3072], P(None, 'dp', 'mp')
- ffn_second: float32 [2, 768, 3072], P(None, 'dp', 'mp'), as said below
- ffn_average: float32 [2, 768, 3072], P(None, 'dp', 'mp')
- norm_params: float32 [6, 768], replicated, as said below
- norm_first: float32 [6, 768], replicated
- norm_second: float32 [6, 768], replicated, as said below
- norm_average: float32 [6, 768], replicated, as said below
- col_bias: float32 [4608], P('mp'), may hold values from -1 to 1
- col_first: float32 [4608], P('mp')
- col_second: float32 [4608], P('mp'), as said below
- col_average: float32 [4608], P('mp'), may hold values from -1 to 1
Outputs:
- loss: float32 [1], replicated
- query_grad: float32 [32, 64, 768], P('dp')
- passage_grad: float32 [32, 512, 768], P('dp')
- attn_master_new: float32 [4, 768, 768], P(None, 'dp', 'mp')
- attn_first_new: float32 [4, 768, 768], P(None, 'dp', 'mp')
- attn_second_new: float32 [4, 768, 768], P(None, 'dp', 'mp')
- attn_average_new: float32 [4, 768, 768], P(None, 'dp', 'mp')
- ffn_master_new: float32 [2, 768, 3072], P(None, 'dp', 'mp')
- ffn_first_new: float32 [2, 768, 3072], P(None, 'dp', 'mp')
- ffn_second_new: float32 [2, 768, 3072], P(None, 'dp', 'mp')
- ffn_average_new: float32 [2, 768, 3072], P(None, 'dp', 'mp')
- norm_params_new: float32 [6, 768], replicated
- norm_first_new: float32 [6, 768], replicated
- norm_second_new: float32 [6, 768], replicated
- norm_average_new: float32 [6, 768], replicated
- col_bias_new: float32 [4608], P('mp')
- col_first_new: float32 [4608], P('mp')
- col_second_new: float32 [4608], P('mp')
- col_average_new: float32 [4608], P('mp')
- attn_copy_new: bfloat16 [4, 768, 768], P(None, 'dp', 'mp')
- ffn_copy_new: bfloat16 [2, 768, 3072], P(None, 'dp', 'mp')
Inputs may be any that keep to these rules, and one draw needn't show every extreme that they name: A query's valid tokens are its first query_len tokens; the first 2 queries are full. A passage's valid tokens are its first passage_len tokens; the first 2 passages are full. The three rates of averaging lie in 0.4 to 0.6; both learning rates are positive. `attn_second`: positive. `ffn_second`: positive. `norm_params`: gains positive. `norm_second`: positive. `norm_average`: gains positive. `col_second`: positive.
All inputs are finite; a program needn't handle non-finite values.
Results may differ from a plain program's by a relative error of at most 0.0085.
The roundings to bfloat16 on the way count: a program that leaves them out, or rounds other values in their place, can miss the bound.
Values may be sent and summed in bfloat16 or wider, within the bound.
A program may use at most 192 MiB of HBM per device.

v0:
```python
import jax
import jax.numpy as jnp
from jax import lax
from jax.sharding import PartitionSpec as P

HD = 64


PRECISE = lax.Precision.HIGHEST
NEG_FILL = -1e30
SOFTMAX_TEMPER = 0.02
NORM_EPS = 1e-12
DECAY_WEIGHT = 0.01
ADAM_EPS = 1e-08


def norm_rows(values, gain, shift):
    center = values - jnp.mean(values, axis=-1, keepdims=True)
    spread = jnp.mean(center * center, axis=-1, keepdims=True)
    return center * lax.rsqrt(spread + NORM_EPS) * gain + shift


def gelu_exact(values):
    return jax.nn.gelu(values, approximate=False)


def token_mask(lengths, slots):
    return (jnp.arange(slots)[None, :] < lengths[:, None]).astype(jnp.float32)


def pool_unit(values, mask_rows, lengths):
    pooled = jnp.sum(values * mask_rows[:, :, None], axis=1) / lengths.astype(jnp.float32)[:, None]
    return pooled * lax.rsqrt(jnp.sum(pooled * pooled, axis=1, keepdims=True) + 1e-06)


def masked_scores(heads_q, heads_k, lengths, score_scale):
    similarity_scores = (
        jnp.einsum("bqhe,bkhe->bhqk", heads_q, heads_k, preferred_element_type=jnp.float32)
        * score_scale
    )
    key_valid = (jnp.arange(heads_k.shape[1])[None, :] < lengths[:, None])[:, None, None, :]
    return jnp.where(key_valid, similarity_scores, NEG_FILL)


def attend_block(heads_q, heads_k, heads_v, lengths, score_scale):
    similarity_scores = masked_scores(heads_q, heads_k, lengths, score_scale)
    row_top = jnp.max(similarity_scores, axis=-1, keepdims=True)
    exp_scores = jnp.exp(similarity_scores - row_top)
    row_total = jnp.sum(exp_scores, axis=-1, keepdims=True)
    attn_probs = (exp_scores / row_total).astype(jnp.bfloat16)
    mixed = jnp.einsum("bhqk,bkhe->bqhe", attn_probs, heads_v, preferred_element_type=jnp.float32)
    return (mixed.astype(jnp.bfloat16), (row_top + jnp.log(row_total))[..., 0])


def attend_back(heads_q, heads_k, heads_v, lengths, log_total, grad_out, score_scale):
    similarity_scores = masked_scores(heads_q, heads_k, lengths, score_scale)
    attn_probs = jnp.exp(similarity_scores - log_total[..., None])
    grad_probs = jnp.einsum(
        "bqhe,bkhe->bhqk", grad_out, heads_v, preferred_element_type=jnp.float32
    )
    inner = jnp.sum(attn_probs * grad_probs, axis=-1, keepdims=True)
    grad_scores = (attn_probs * (grad_probs - inner) * score_scale).astype(jnp.bfloat16)
    grad_q = jnp.einsum("bhqk,bkhe->bqhe", grad_scores, heads_k, preferred_element_type=jnp.float32)
    grad_k = jnp.einsum("bhqk,bqhe->bkhe", grad_scores, heads_q, preferred_element_type=jnp.float32)
    grad_v = jnp.einsum(
        "bhqk,bqhe->bkhe",
        attn_probs.astype(jnp.bfloat16),
        grad_out,
        preferred_element_type=jnp.float32,
    )
    return (grad_q.astype(jnp.bfloat16), grad_k.astype(jnp.bfloat16), grad_v.astype(jnp.bfloat16))


def adam_update(master, first, second, average, grad, rate, decay_w, rates, step_count):
    first_new = rates[0] * first + (1.0 - rates[0]) * grad
    second_new = rates[1] * second + (1.0 - rates[1]) * grad * grad
    fixed_one = first_new / (1.0 - rates[0] ** step_count)
    fixed_two = second_new / (1.0 - rates[1] ** step_count)
    master_new = master - rate * (fixed_one / (jnp.sqrt(fixed_two) + ADAM_EPS) + decay_w * master)
    average_new = rates[2] * average + (1.0 - rates[2]) * master_new
    return (master_new, first_new, second_new, average_new)


def per_device(
    query_in,
    passage_in,
    query_len,
    passage_len,
    positive,
    step,
    rates,
    attn_master,
    attn_first,
    attn_second,
    attn_average,
    ffn_master,
    ffn_first,
    ffn_second,
    ffn_average,
    norm_params,
    norm_first,
    norm_second,
    norm_average,
    col_bias,
    col_first,
    col_second,
    col_average,
):
    count_of_pairs = query_in.shape[0]
    query_slots = query_in.shape[1]
    passage_slots = passage_in.shape[1]
    model_width = query_in.shape[2]
    query_rows = count_of_pairs * query_slots
    attn_w, ffn_w = (
        lax.all_gather(attn_master.astype(jnp.bfloat16), "dp", axis=1, tiled=True),
        lax.all_gather(ffn_master.astype(jnp.bfloat16), "dp", axis=1, tiled=True),
    )
    local_width = attn_w.shape[2]
    local_heads = local_width // HD
    score_scale = HD ** (-0.5)
    query_bias = col_bias[:local_width]
    value_bias = col_bias[local_width : 2 * local_width]
    hidden_bias = col_bias[2 * local_width :]
    tokens = jnp.concatenate(
        [query_in.reshape(-1, model_width), passage_in.reshape(-1, model_width)], axis=0
    )
    projected = jnp.einsum("td,sde->ste", tokens, attn_w[:3], preferred_element_type=jnp.float32)
    proj_q = (projected[0] + query_bias).astype(jnp.bfloat16)
    proj_k = projected[1].astype(jnp.bfloat16)
    proj_v = (projected[2] + value_bias).astype(jnp.bfloat16)

    def split_heads(values):
        return (
            values[:query_rows].reshape(count_of_pairs, query_slots, local_heads, HD),
            values[query_rows:].reshape(count_of_pairs, passage_slots, local_heads, HD),
        )

    query_q, passage_q = split_heads(proj_q)
    query_k, passage_key = split_heads(proj_k)
    query_v, passage_v = split_heads(proj_v)
    out_query, total_query = attend_block(query_q, query_k, query_v, query_len, score_scale)

    def passage_forward(passage_item):
        one_q, one_k, one_v, one_len = passage_item
        one_out, one_total = attend_block(
            one_q[None], one_k[None], one_v[None], one_len[None], score_scale
        )
        return (one_out[0], one_total[0])

    out_passage, total_passage = lax.map(
        passage_forward, (passage_q, passage_key, passage_v, passage_len)
    )
    mixed_heads = jnp.concatenate(
        [out_query.reshape(-1, local_width), out_passage.reshape(-1, local_width)], axis=0
    )
    branch_part = lax.dot_general(
        mixed_heads, attn_w[3], (((1,), (1,)), ((), ())), preferred_element_type=jnp.float32
    )
    branch = lax.psum(branch_part, "mp")
    z_one = tokens.astype(jnp.float32) + branch + norm_params[0]
    first_norm = norm_rows(z_one, norm_params[1], norm_params[2])
    first_low = first_norm.astype(jnp.bfloat16)
    hidden = jnp.dot(first_low, ffn_w[0], preferred_element_type=jnp.float32) + hidden_bias
    active = gelu_exact(hidden).astype(jnp.bfloat16)
    ffn_part = lax.dot_general(
        active, ffn_w[1], (((1,), (1,)), ((), ())), preferred_element_type=jnp.float32
    )
    branch_two = lax.psum(ffn_part, "mp")
    z_two = first_norm + branch_two + norm_params[3]
    query_mask = token_mask(query_len, query_slots)
    passage_mask = token_mask(passage_len, passage_slots)

    def pooled_tail(values, gain, shift):
        normed = norm_rows(values, gain, shift)
        return (
            pool_unit(
                normed[:query_rows].reshape(count_of_pairs, query_slots, model_width),
                query_mask,
                query_len,
            ),
            pool_unit(
                normed[query_rows:].reshape(count_of_pairs, passage_slots, model_width),
                passage_mask,
                passage_len,
            ),
        )

    (unit_q, unit_p), tail_pull = jax.vjp(pooled_tail, z_two, norm_params[4], norm_params[5])
    every_unit = lax.all_gather(unit_p, "dp", axis=0, tiled=True)
    total_pairs = count_of_pairs * lax.axis_size("dp")
    similarity_scores = (
        jnp.dot(unit_q, every_unit.T, precision=PRECISE, preferred_element_type=jnp.float32)
        / SOFTMAX_TEMPER
    )
    row_top = jnp.max(similarity_scores, axis=1, keepdims=True)
    exp_scores = jnp.exp(similarity_scores - row_top)
    row_total = jnp.sum(exp_scores, axis=1, keepdims=True)
    log_total = row_top[:, 0] + jnp.log(row_total[:, 0])
    target = (jnp.arange(total_pairs)[None, :] == positive[:, None]).astype(jnp.float32)
    part_loss = jnp.sum(log_total - jnp.sum(similarity_scores * target, axis=1))
    loss_value = lax.psum(part_loss.reshape(1), "dp") / total_pairs
    grad_scores = (exp_scores / row_total - target) / total_pairs
    grad_uq = (
        jnp.dot(grad_scores, every_unit, precision=PRECISE, preferred_element_type=jnp.float32)
        / SOFTMAX_TEMPER
    )
    grad_every = (
        jnp.dot(grad_scores.T, unit_q, precision=PRECISE, preferred_element_type=jnp.float32)
        / SOFTMAX_TEMPER
    )
    grad_up = lax.psum_scatter(grad_every, "dp", scatter_dimension=0, tiled=True)
    grad_ztwo, grad_gain_two, grad_shift_two = tail_pull((grad_uq, grad_up))
    grad_bias_two = jnp.sum(grad_ztwo, axis=0)
    grad_branch_two = grad_ztwo.astype(jnp.bfloat16)
    grad_active = jnp.dot(grad_branch_two, ffn_w[1], preferred_element_type=jnp.float32)
    grad_w_down = lax.dot_general(
        grad_branch_two, active, (((0,), (0,)), ((), ())), preferred_element_type=jnp.float32
    )
    _, gelu_pull = jax.vjp(gelu_exact, hidden)
    grad_hidden = gelu_pull(grad_active)[0].astype(jnp.bfloat16)
    grad_hidden_bias = jnp.sum(grad_hidden.astype(jnp.float32), axis=0)
    grad_w_up = lax.dot_general(
        first_low, grad_hidden, (((0,), (0,)), ((), ())), preferred_element_type=jnp.float32
    )
    first_part = lax.dot_general(
        grad_hidden, ffn_w[0], (((1,), (1,)), ((), ())), preferred_element_type=jnp.float32
    )
    grad_first = lax.psum(first_part, "mp") + grad_ztwo
    _, first_pull = jax.vjp(norm_rows, z_one, norm_params[1], norm_params[2])
    grad_zone, grad_gain_one, grad_shift_one = first_pull(grad_first)
    grad_bias_out = jnp.sum(grad_zone, axis=0)
    grad_branch = grad_zone.astype(jnp.bfloat16)
    grad_w_out = lax.dot_general(
        grad_branch, mixed_heads, (((0,), (0,)), ((), ())), preferred_element_type=jnp.float32
    )
    grad_mixed = jnp.dot(grad_branch, attn_w[3], preferred_element_type=jnp.float32).astype(
        jnp.bfloat16
    )
    grad_mixed_q = grad_mixed[:query_rows].reshape(count_of_pairs, query_slots, local_heads, HD)
    grad_mixed_p = grad_mixed[query_rows:].reshape(count_of_pairs, passage_slots, local_heads, HD)
    back_q = attend_back(
        query_q, query_k, query_v, query_len, total_query, grad_mixed_q, score_scale
    )

    def passage_backward(passage_item):
        one_q, one_k, one_v, one_len, one_total, one_grad = passage_item
        grads_one = attend_back(
            one_q[None],
            one_k[None],
            one_v[None],
            one_len[None],
            one_total[None],
            one_grad[None],
            score_scale,
        )
        return (grads_one[0][0], grads_one[1][0], grads_one[2][0])

    back_p = lax.map(
        passage_backward,
        (passage_q, passage_key, passage_v, passage_len, total_passage, grad_mixed_p),
    )
    grad_proj = jnp.stack(
        [
            jnp.concatenate(
                [back_q[index].reshape(-1, local_width), back_p[index].reshape(-1, local_width)],
                axis=0,
            )
            for index in range(3)
        ]
    )
    grad_w_qkv = jnp.einsum("td,ste->sde", tokens, grad_proj, preferred_element_type=jnp.float32)
    grad_query_bias = jnp.sum(grad_proj[0].astype(jnp.float32), axis=0)
    grad_value_bias = jnp.sum(grad_proj[2].astype(jnp.float32), axis=0)
    input_part = jnp.einsum(
        "ste,sde->td", grad_proj, attn_w[:3], preferred_element_type=jnp.float32
    )
    grad_tokens = lax.psum(input_part, "mp") + grad_zone
    attn_grad_full = jnp.concatenate([grad_w_qkv, grad_w_out[None]], axis=0)
    attn_grad, ffn_grad = (
        lax.psum_scatter(attn_grad_full, "dp", scatter_dimension=1, tiled=True),
        lax.psum_scatter(
            jnp.stack([grad_w_up, grad_w_down]), "dp", scatter_dimension=1, tiled=True
        ),
    )
    norm_grad_part = jnp.stack(
        [grad_bias_out, grad_gain_one, grad_shift_one, grad_bias_two, grad_gain_two, grad_shift_two]
    )
    col_grad_part = jnp.concatenate([grad_query_bias, grad_value_bias, grad_hidden_bias])
    norm_grad, column_gradient = lax.psum((norm_grad_part, col_grad_part), "dp")
    step_count = step[0].astype(jnp.float32)
    attn_out = adam_update(
        attn_master,
        attn_first,
        attn_second,
        attn_average,
        attn_grad,
        rates[3],
        DECAY_WEIGHT,
        rates,
        step_count,
    )
    ffn_out = adam_update(
        ffn_master,
        ffn_first,
        ffn_second,
        ffn_average,
        ffn_grad,
        rates[3],
        DECAY_WEIGHT,
        rates,
        step_count,
    )
    norm_out = adam_update(
        norm_params,
        norm_first,
        norm_second,
        norm_average,
        norm_grad,
        rates[4],
        0.0,
        rates,
        step_count,
    )
    col_out = adam_update(
        col_bias,
        col_first,
        col_second,
        col_average,
        column_gradient,
        rates[4],
        0.0,
        rates,
        step_count,
    )
    query_grad = grad_tokens[:query_rows].reshape(count_of_pairs, query_slots, model_width)
    passage_grad = grad_tokens[query_rows:].reshape(count_of_pairs, passage_slots, model_width)
    return (
        loss_value,
        query_grad,
        passage_grad,
        attn_out[0],
        attn_out[1],
        attn_out[2],
        attn_out[3],
        ffn_out[0],
        ffn_out[1],
        ffn_out[2],
        ffn_out[3],
        norm_out[0],
        norm_out[1],
        norm_out[2],
        norm_out[3],
        col_out[0],
        col_out[1],
        col_out[2],
        col_out[3],
        attn_out[0].astype(jnp.bfloat16),
        ffn_out[0].astype(jnp.bfloat16),
    )


def solution(mesh):
    placed = (
        P("dp", None, None),
        P("dp", None, None),
        P("dp"),
        P("dp"),
        P("dp"),
        P(),
        P(),
        P(None, "dp", "mp"),
        P(None, "dp", "mp"),
        P(None, "dp", "mp"),
        P(None, "dp", "mp"),
        P(None, "dp", "mp"),
        P(None, "dp", "mp"),
        P(None, "dp", "mp"),
        P(None, "dp", "mp"),
        P(),
        P(),
        P(),
        P(),
        P("mp"),
        P("mp"),
        P("mp"),
        P("mp"),
    )
    return jax.shard_map(
        per_device,
        mesh=mesh,
        in_specs=placed,
        out_specs=(
            P(),
            P("dp", None, None),
            P("dp", None, None),
            P(None, "dp", "mp"),
            P(None, "dp", "mp"),
            P(None, "dp", "mp"),
            P(None, "dp", "mp"),
            P(None, "dp", "mp"),
            P(None, "dp", "mp"),
            P(None, "dp", "mp"),
            P(None, "dp", "mp"),
            P(),
            P(),
            P(),
            P(),
            P("mp"),
            P("mp"),
            P("mp"),
            P("mp"),
            P(None, "dp", "mp"),
            P(None, "dp", "mp"),
        ),
        check_vma=False,
    )
```

profile of v0, /device:TPU:0, one launch (start us, length us, event | category | flops | bytes accessed | tf_op | source)
XLA Modules:
  0.0 1049.0 jit_solution(2143462107333688623)
XLA Ops:
  11.0 65.4 %all-gather.4.cloned.1.call-done = bf16[4,768,384]{2,1,0:T(8,128)(2,1)} async-done(((bf16[4,48,384]{2,1,0:T(8,128)(2,1)}), bf16[4,768,384]{2,1,0:T(8,128)(2,1)}) %all-gather.4.cloned.1.call-update) | async-done | bytes 2359312 | tf_op jit(solution)/shard_map/all_gather | solution.py:115
  76.4 4.5 fusion.199
  90.6 3.5 reshape.440
  96.5 2.6 reshape.441
  102.3 12.0 %while.26 = (s32[]{:T(128)}, bf16[2,512,6,64]{1,3,2,0:T(8,128)(2,1)S(1)}, f32[2,6,512]{2,1,0:T(8,128)S(1)}, bf16[2,512,6,64]{1,3,2,0:T(8,128)(2,1)S(1)}, s32[2]{...) while((s32[]{:T(128)}, ...), condition=%wide.region_5.6_spmd, body=%wide.region_2.5_spmd.sunk | while | flops 421721600 | bytes 20570216 | solution.py:150
  116.2 4.3 fusion.143
  123.2 20.3 %all-reduce.12.cloned.1.call-done = f32[1152,768]{1,0:T(8,128)} async-done(((f32[1152,768]{1,0:T(8,128)}), f32[1152,768]{1,0:T(8,128)}) %all-reduce.12.cloned.1.call-update) | async-done | bytes 3538960 | tf_op jit(solution)/shard_map/psum | solution.py:159
  143.5 3.0 fusion.196
  147.7 81.2 %all-gather.6.cloned.1.call-done = bf16[2,768,1536]{2,1,0:T(8,128)(2,1)} async-done(((bf16[2,48,1536]{2,1,0:T(8,128)(2,1)}), bf16[2,768,1536]{2,1,0:T(8,128)(2,1)}) %all-gather.6.cloned.1.call-update) | async-done | bytes 4718608 | tf_op jit(solution)/shard_map/all_gather | solution.py:116
  228.8 21.7 %multiply_convert_fusion.1 = (bf16[1152,1536]{1,0:T(8,128)(2,1)S(1)}, f32[1152,1536]{1,0:T(8,128)}, f32[1152,1536]{1,0:T(8,128)}) fusion(f32[1536]{0:T(1024)} %slice.154, bf16[2,768,1536]{2,1,0:T(8,128)(2,1)} %all-gather.6.cloned.1.call-done, f32[1152,768]{1,0:T(8,128)S(1)} %get-tuple-element.330, f32[768]{0:T(1024)} %get-tuple-element.257, ...), kind=kOutput, calls=%fused_computation.87 | convolution fusion | flops 2839117824 | bytes 23618560 | tf_op jit(solution)/shard_map/dot_general | solution.py:163
  252.4 4.8 fusion.117
  264.8 15.2 %all-reduce.14.cloned.1.call-done = f32[1152,768]{1,0:T(8,128)} async-done(((f32[1152,768]{1,0:T(8,128)}), f32[1152,768]{1,0:T(8,128)}) %all-reduce.14.cloned.1.call-update) | async-done | bytes 3538960 | tf_op jit(solution)/shard_map/psum | solution.py:168
  280.0 3.1 fusion.194
  287.2 43.8 %all-gather = f32[16,2,768]{2,1,0:T(2,128)} all-gather(f32[1,2,768]{2,1,0:T(2,128)S(1)} %multiply_bitcast_fusion), channel_id=1, replica_groups=mesh['dp'=16,'mp'=2] {'dp'}, dimensions={0}, use_global_device_ids=true | all-gather | bytes 104448 | tf_op jit(solution)/shard_map/all_gather | solution.py:189
  338.9 2.4 multiply_reduce_fusion.10
  344.4 96.2 %all-reduce.20.cloned.1.call-done = f32[32,768]{1,0:T(8,128)} async-done(((f32[32,768]{1,0:T(8,128)}), f32[32,768]{1,0:T(8,128)}) %all-reduce.20.cloned.1.call-update) | async-done | bytes 98320
  443.9 4.1 multiply_reduce_fusion.1
  449.4 10.1 convert_reduce_fusion
  461.3 4.7 fusion.115
  467.4 22.8 %all-reduce.16.cloned.1.call-done = f32[1152,768]{1,0:T(8,128)} async-done(((f32[1152,768]{1,0:T(8,128)}), f32[1152,768]{1,0:T(8,128)}) %all-reduce.16.cloned.1.call-update) | async-done | bytes 3538960 | tf_op jit(solution)/shard_map/psum | solution.py:228
  490.2 5.9 multiply_reduce_fusion.2
  499.2 2.2 convolution_convert_fusion
  506.6 1.9 fusion.158
  508.5 2.0 fusion.135
  510.5 2.5 fusion.133
  512.9 2.5 fusion.134
  519.1 2.3 copy.222
  521.3 3.2 reshape.449
  524.6 2.1 copy.225
  529.6 84.5 %while.27 = (s32[]{:T(128)}, bf16[2,512,6,64]{1,3,2,0:T(8,128)(2,1)}, bf16[2,512,6,64]{1,3,2,0:T(8,128)(2,1)}, bf16[2,512,6,64]{1,3,2,0:T(8,128)(2,1)}, bf16[2,5...) while((s32[]{:T(128)}, ...), condition=%wide.region_32.33_spmd, body=%wide.region_30.32_spmd.sunk | while | flops 1048124928 | bytes 79642896 | solution.py:258
  529.9 4.9 fusion.250
  534.8 3.7 fusion.249
  540.8 13.0 %fusion.252 = bf16[2,512,6,64]{1,3,2,0:T(8,128)(2,1)} fusion(bf16[2,512,6,64]{1,3,2,0:T(8,128)(2,1)} %get-tuple-element.511, s32[]{:T(128)} %get-tuple-element.509, f32[6,512,512]{1,2,0:T(8,128)} %fusion.249, f32[6,512,512]{1,2,0:T(8,128)} %fusion.250, f32[6,512]{1,0:T(8,128)} %dynamic-slice_bitcast_fusion.2, pred[512]{0:T(512)(128)(4,1)} %iota_compare_fusion.7, ...), kind=kOutput, calls=%fused_computation.44.clone.1 | convolution fusion | flops 218828288 | bytes 25987072 | tf_op jit(solution)/shard_map/while/body/eval_jaxpr/bhqk,bqhe->bkhe/dot_general | solution.py:64
  553.9 12.8 %fusion.251 = bf16[2,512,6,64]{1,3,2,0:T(8,128)(2,1)} fusion(bf16[2,512,6,64]{1,3,2,0:T(8,128)(2,1)} %get-tuple-element.510, s32[]{:T(128)} %get-tuple-element.509, f32[6,512,512]{1,2,0:T(8,128)} %fusion.249, f32[6,512,512]{1,2,0:T(8,128)} %fusion.250, f32[6,512]{1,0:T(8,128)} %dynamic-slice_bitcast_fusion.2, pred[512]{0:T(512)(128)(4,1)} %iota_compare_fusion.7, ...), kind=kOutput, calls=%fused_computation.46.clone.1 | convolution fusion | flops 218828288 | bytes 25987072 | tf_op jit(solution)/shard_map/while/body/eval_jaxpr/bhqk,bkhe->bqhe/dot_general | solution.py:63
  566.7 5.2 fusion.253
  571.9 4.9 fusion.250
  576.8 3.7 fusion.249
  582.9 13.0 %fusion.252 = bf16[2,512,6,64]{1,3,2,0:T(8,128)(2,1)} fusion(bf16[2,512,6,64]{1,3,2,0:T(8,128)(2,1)} %get-tuple-element.511, s32[]{:T(128)} %get-tuple-element.509, f32[6,512,512]{1,2,0:T(8,128)} %fusion.249, f32[6,512,512]{1,2,0:T(8,128)} %fusion.250, f32[6,512]{1,0:T(8,128)} %dynamic-slice_bitcast_fusion.2, pred[512]{0:T(512)(128)(4,1)} %iota_compare_fusion.7, ...), kind=kOutput, calls=%fused_computation.44.clone.1 | convolution fusion | flops 218828288 | bytes 25987072 | tf_op jit(solution)/shard_map/while/body/eval_jaxpr/bhqk,bqhe->bkhe/dot_general | solution.py:64
  595.9 12.8 %fusion.251 = bf16[2,512,6,64]{1,3,2,0:T(8,128)(2,1)} fusion(bf16[2,512,6,64]{1,3,2,0:T(8,128)(2,1)} %get-tuple-element.510, s32[]{:T(128)} %get-tuple-element.509, f32[6,512,512]{1,2,0:T(8,128)} %fusion.249, f32[6,512,512]{1,2,0:T(8,128)} %fusion.250, f32[6,512]{1,0:T(8,128)} %dynamic-slice_bitcast_fusion.2, pred[512]{0:T(512)(128)(4,1)} %iota_compare_fusion.7, ...), kind=kOutput, calls=%fused_computation.46.clone.1 | convolution fusion | flops 218828288 | bytes 25987072 | tf_op jit(solution)/shard_map/while/body/eval_jaxpr/bhqk,bkhe->bqhe/dot_general | solution.py:63
  608.7 5.1 fusion.253
  614.2 1.9 copy.227
  617.1 2.3 copy.229
  626.7 1.9 copy.233
  629.6 2.3 copy.235
  631.9 1.9 copy.239
  634.9 2.3 copy.241
  641.7 4.3 convolution_bitcast_fusion.3
  646.2 3.4 convolution_bitcast_fusion.5
  649.7 2.6 convolution_bitcast_fusion.4
  652.3 2.8 pad_maximum_fusion.1
  655.1 6.7 copy.244
  662.1 6.7 convolution_bitcast_fusion.1
  668.8 3.8 convolution_bitcast_fusion.2
  672.6 4.5 pad_maximum_fusion
  690.7 4.3 add_add_fusion.4
  695.8 80.2 %all-reduce.4 = (f32[1]{0:T(128)}, f32[6,768]{1,0:T(8,128)S(1)}, f32[2304]{0:T(1024)S(1)}) all-reduce(f32[1]{0:T(128)} %bitcast.32, f32[6,768]{1,0:T(8,128)S(1)} %stack.43, f32[2304]{0:T(1024)S(1)} %pad_maximum_fusion.10), channel_id=1, replica_groups=mesh['dp'=16,'mp'=2] {'dp'}, use_global_device_ids=true, to_apply=%region_20.21 | all-reduce | flops 6913 | bytes 55304 | tf_op jit(solution)/shard_map/psum | solution.py:201
  776.1 3.8 slice.187
  782.5 3.2 multiply_add_fusion.8
  785.7 3.2 multiply_add_fusion.6
  788.9 69.7 %all-reduce.22.cloned.1.call-done = f32[4,768,384]{2,0,1:T(4,128)} async-done(((f32[4,768,384]{2,0,1:T(4,128)}), f32[4,768,384]{2,0,1:T(4,128)}) %all-reduce.22.cloned.1.call-update) | async-done | bytes 4718608
  859.7 3.9 fusion.188
  863.6 2.3 multiply_add_fusion.4
  865.9 169.4 %reduce-scatter.2.cloned.1.call-done = f32[2,48,1536]{2,1,0:T(8,128)} async-done(((f32[2,768,1536]{2,1,0:T(8,128)}), f32[2,48,1536]{2,1,0:T(8,128)}) %reduce-scatter.2.cloned.1.call-update) | async-done | bytes 589840 | tf_op jit(solution)/shard_map/reduce_scatter | solution.py:281
  1035.3 4.4 fusion.186
  (324 shorter events, 116.5 us)
Async XLA Ops:
  7.2 69.2 %all-gather.4.cloned.1.call-start = ((), (), s32[]{:S(2)}) async-start(), calls=%async_computation.1 | async-start | bytes 2506752 | tf_op jit(solution)/shard_map/all_gather | solution.py:115
  8.9 134.6 %all-reduce.12.cloned.1.call-start = ((), (), s32[]{:S(2)}) async-start(), calls=%async_computation.2 | async-start | bytes 7077888 | tf_op jit(solution)/shard_map/psum | solution.py:159
  83.0 6.5 copy-start.15
  86.3 9.0 copy-start.28
  87.7 7.6 copy-start.14
  114.2 6.3 copy-start.3
  114.3 6.3 copy-start.4
  114.3 6.3 copy-start.7
  114.3 6.2 copy-start.37
  116.2 4.5 copy-start.17
  120.6 108.3 %all-gather.6.cloned.1.call-start = ((), (), s32[]{:S(2)}) async-start(), calls=%async_computation.3 | async-start | bytes 5013504 | tf_op jit(solution)/shard_map/all_gather | solution.py:116
  121.4 158.6 %all-reduce.14.cloned.1.call-start = ((), (), s32[]{:S(2)}) async-start(), calls=%async_computation.4 | async-start | bytes 7077888 | tf_op jit(solution)/shard_map/psum | solution.py:168
  228.8 23.6 %copy-start.83 = (bf16[2,768,1536]{2,1,0:T(8,128)(2,1)S(1)}, bf16[2,768,1536]{2,1,0:T(8,128)(2,1)}, u32[]{:S(2)}) copy-start(bf16[2,768,1536]{2,1,0:T(8,128)(2,1)} %all-gather.6.cloned.1.call-done) | copy-start | bytes 14155780
  257.2 183.3 %all-reduce.20.cloned.1.call-start = ((), (), s32[]{:S(2)}) async-start(), calls=%async_computation.8 | async-start | bytes 196608
  341.4 148.8 %all-reduce.16.cloned.1.call-start = ((), (), s32[]{:S(2)}) async-start(), calls=%async_computation.5 | async-start | bytes 7077888 | tf_op jit(solution)/shard_map/psum | solution.py:228
  443.8 4.2 copy-start.52
  443.8 4.2 copy-start.1
  443.8 4.2 copy-start.10
  443.8 4.2 copy-start.40
  443.8 4.2 copy-start.44
  443.8 4.2 copy-start.54
  443.8 5.5 slice-start
  449.3 10.2 copy-start.2
  449.4 10.2 copy-start.32
  466.0 224.7 %all-reduce.18.cloned.1.call-start = ((), (), s32[]{:S(2)}) async-start(), calls=%async_computation.6 | async-start | bytes 7077888 | tf_op jit(solution)/shard_map/psum | solution.py:277
  490.2 5.9 copy-start.50
  490.2 5.9 copy-start.33
  497.4 4.0 copy-start.59
  529.8 4.9 copy-start.8
  529.8 4.9 copy-start.9
  534.8 3.7 copy-start.38
  534.8 4.3 copy-start.81
  571.9 4.9 copy-start.8
  571.9 4.9 copy-start.9
  576.8 3.7 copy-start.38
  576.8 4.3 copy-start.81
  637.2 4.5 copy-start.42
  646.1 212.6 %all-reduce.22.cloned.1.call-start = ((), (), s32[]{:S(2)}) async-start(), calls=%async_computation.9 | async-start | bytes 9437184
  646.2 3.5 copy-start.41
  661.8 373.4 %reduce-scatter.2.cloned.1.call-start = ((), (), s32[]{:S(2)}) async-start(), calls=%async_computation.7 | async-start | bytes 10027008 | tf_op jit(solution)/shard_map/reduce_scatter | solution.py:281
  662.0 6.7 copy-start.13
  662.1 6.7 copy-start.34
  662.1 6.7 copy-start.36
  677.0 7.6 copy-start.64
  677.0 8.2 copy-start.63
  677.1 10.1 copy-start.68
  677.1 10.6 %copy-start.67 = (f32[768]{0:T(1024)S(1)}, f32[768]{0:T(1024)}, u32[]{:S(2)}) copy-start(f32[768]{0:T(1024)} %get-tuple-element.337) | copy-start | bytes 9220
  677.1 13.6 %copy-start.6 = (f32[1152,768]{1,0:T(8,128)S(1)}, f32[1152,768]{1,0:T(8,128)}, u32[]{:S(2)}) copy-start(f32[1152,768]{1,0:T(8,128)} %copy-done.5) | copy-start | bytes 10616836
  690.7 4.4 copy-start.72
  776.0 6.5 copy-start.57
  776.0 6.5 copy-start.69
  776.0 6.5 copy-start.70
  776.0 6.5 copy-start.71
  776.0 9.7 copy-start.47
  776.0 9.7 copy-start.60
  776.0 9.7 copy-start.61
  776.0 9.7 copy-start.62
  776.1 83.6 %copy-start.20 = (f32[4,48,384]{2,1,0:T(8,128)S(1)}, f32[4,48,384]{2,1,0:T(8,128)}, u32[]{:S(2)}) copy-start(f32[4,48,384]{2,1,0:T(8,128)} %param.34) | copy-start | bytes 884740
  776.1 83.6 %copy-start.35 = (f32[4,48,384]{2,1,0:T(8,128)S(1)}, f32[4,48,384]{2,1,0:T(8,128)}, u32[]{:S(2)}) copy-start(f32[4,48,384]{2,1,0:T(8,128)} %param.36) | copy-start | bytes 884740
  779.9 255.4 %copy-start.18 = (f32[2,48,1536]{2,1,0:T(8,128)S(1)}, f32[2,48,1536]{2,1,0:T(8,128)}, u32[]{:S(2)}) copy-start(f32[2,48,1536]{2,1,0:T(8,128)} %param.38) | copy-start | bytes 1769476
  779.9 255.4 %copy-start.29 = (f32[2,48,1536]{2,1,0:T(8,128)S(1)}, f32[2,48,1536]{2,1,0:T(8,128)}, u32[]{:S(2)}) copy-start(f32[2,48,1536]{2,1,0:T(8,128)} %param.40) | copy-start | bytes 1769476
  779.9 255.4 %copy-start.30 = (f32[2,48,1536]{2,1,0:T(8,128)S(1)}, f32[2,48,1536]{2,1,0:T(8,128)}, u32[]{:S(2)}) copy-start(f32[2,48,1536]{2,1,0:T(8,128)} %param.39) | copy-start | bytes 1769476
  859.7 180.0 %copy-start.31 = (f32[2,48,1536]{2,1,0:T(8,128)S(1)}, f32[2,48,1536]{2,1,0:T(8,128)}, u32[]{:S(2)}) copy-start(f32[2,48,1536]{2,1,0:T(8,128)} %param.41) | copy-start | bytes 1769476
  863.6 177.6 %copy-start.21 = (f32[4,48,384]{2,1,0:T(8,128)}, f32[4,48,384]{2,1,0:T(8,128)S(1)}, u32[]{:S(2)}) copy-start(f32[4,48,384]{2,1,0:T(8,128)S(1)} %get-tuple-element.305) | copy-start | bytes 884740
  (35 other events, 54.8 us)
Sparse Core Ops, SparseCore 0:
  11.3 65.0 all-gather.3
  120.7 22.7 all-reduce.11
  147.2 81.6 all-gather.5
  257.3 22.6 all-reduce.13
  341.5 99.0 all-reduce.19
  466.1 23.9 all-reduce.15
  646.2 25.1 all-reduce.17
  677.1 181.5 all-reduce.21
  865.3 169.9 reduce-scatter.1
where the time goes:
time: 1060 us; the launch traced here: 1050 us
  waiting for transfers between devices  540 us (51%)
  matrix products  175 us (17%)
  blocking collectives  124 us (12%)
  local copies, waits for them, and re-layouts  103 us (10%)
  other arithmetic  82.7 us (8%)
  between operations  22.3 us (2%)
    reduce_scatter x1, waiting for transfers between devices, per_device(): lax.psum_scatter(jnp.stack([grad_w_up, grad_w_down]), 'dp', scatter_dimen...  169 us
    unnamed x11, waiting for transfers between devices  166 us
    all_gather x1, waiting for transfers between devices, per_device(): lax.all_gather(ffn_master.astype(jnp.bfloat16), 'dp', axis=1, tiled=True)  81.2 us
    psum x1, blocking collectives, per_device(): loss_value = lax.psum(part_loss.reshape(1), 'dp') / total_pairs  80.2 us
    all_gather x1, waiting for transfers between devices, per_device(): lax.all_gather(attn_master.astype(jnp.bfloat16), 'dp', axis=1, tiled=True)  65.4 us
    all_gather x1, blocking collectives, per_device(): every_unit = lax.all_gather(unit_p, 'dp', axis=0, tiled=True)  43.8 us
    dot_general x3, matrix products, attend_back(): jnp.einsum('bhqk,bqhe->bkhe', grad_scores, heads_q, preferred_element_typ...  28.5 us
    dot_general x3, matrix products, attend_back(): jnp.einsum('bhqk,bkhe->bqhe', grad_scores, heads_k, preferred_element_typ...  28.1 us
  transfers between devices with their start and end apart: 9, of which 8 were waited for; matrix products, arithmetic and copies ran while one was open for 8% of the time, Pallas kernels for 0%

commit v1 on v0

v1 whole, which is shorter than its diff:
```python
import functools

import jax
import jax.numpy as jnp
from jax import lax
from jax.experimental import pallas as pl
from jax.experimental.pallas import tpu as pltpu
from jax.sharding import PartitionSpec as P

HD = 64
LANES = 128
NEG_FILL = -1e30
SOFTMAX_TEMPER = 0.02
NORM_EPS = 1e-12
POOL_EPS = 1e-06
DECAY_WEIGHT = 0.01
ADAM_EPS = 1e-08
PRECISE = lax.Precision.HIGHEST
MESH = pl.DeviceIdType.MESH
MIB = 2**20
F32 = jnp.float32
BF16 = jnp.bfloat16

ERFC_STEP = 0.46
ERFC_HALF = (
    0.5 * 0.26113873056821263,
    0.5 * 0.23637801512084577,
    0.5 * 0.3601812301921897,
    -0.5 * 0.18740624158431016,
    0.5 * 0.6751549397754679,
    -0.5 * 0.4305350150859377,
    0.5 * 0.0850883282904581,
)
ROOT_HALF = 0.7071067811865476
DENSITY = 0.3989422804014327


def gelu_and_slope(hidden):
    bell = jnp.exp(hidden * hidden * (-0.5))
    step = 1.0 / (1.0 + (ERFC_STEP * ROOT_HALF) * jnp.abs(hidden))
    tail = ERFC_HALF[6]
    for coefficient in ERFC_HALF[5::-1]:
        tail = tail * step + coefficient
    tail = tail * step * bell
    below = jnp.where(hidden >= 0.0, 1.0 - tail, tail)
    return hidden * below, below + hidden * bell * DENSITY


def mm(left, right):
    return jnp.dot(left, right, preferred_element_type=F32)


def mm_nt(left, right):
    return lax.dot_general(left, right, (((1,), (1,)), ((), ())), preferred_element_type=F32)


def mm_tn(left, right):
    return lax.dot_general(left, right, (((0,), (0,)), ((), ())), preferred_element_type=F32)


def gather_kernel(
    attn_ref, ffn_ref, col_ref, attn_own, ffn_own, attn_oth, ffn_oth, col_oth,
    z_send, z_recv, x_send, x_recv, y_send, y_recv, d_send, d_recv, c_send, c_recv, b_send, b_recv, here_sem,
):
    me = lax.axis_index("dp")
    core = lax.axis_index("mp")
    x, y, z = lax.rem(me, 2), lax.rem(me // 2, 2), me // 4
    rows = attn_ref.shape[1]
    half = ffn_ref.shape[2] // 2

    def index_of(zz, yy, xx):
        return (zz * 2 + yy) * 2 + xx

    column = [lax.rem(z - k + 4, 4) for k in range(4)]
    z_peer = [None] + [(index_of(lax.rem(z + k, 4), y, x), core) for k in range(1, 4)]
    x_peer = (index_of(z, y, 1 - x), core)
    y_peer = (index_of(z, 1 - y, x), core)
    c_peer = (me, 1 - core)

    barrier = pltpu.get_barrier_semaphore()
    for peer in [*z_peer[1:], x_peer, y_peer, c_peer]:
        pl.semaphore_signal(barrier, inc=1, device_id=peer, device_id_type=MESH)
    pl.semaphore_wait(barrier, 6)

    def span(index, count=1):
        return pl.ds(pl.multiple_of(index * rows, rows), count * rows)

    def whole(chunk, index, count=1, other=False):
        if chunk == 0:
            return (attn_oth if other else attn_own).at[:, span(index, count), :]
        return (ffn_oth if other else ffn_own).at[chunk - 1, span(index, count), :]

    def part(chunk, index, which):
        if chunk == 0:
            return attn_own.at[pl.ds(2 * which, 2), span(index), :]
        return ffn_own.at[chunk - 1, span(index), pl.ds(which * half, half)]

    def mine(chunk):
        return attn_ref if chunk == 0 else ffn_ref.at[chunk - 1]

    sends = []

    def push(source, target, send, recv, peer):
        copy = pltpu.make_async_remote_copy(
            src_ref=source, dst_ref=target, send_sem=send, recv_sem=recv, device_id=peer, device_id_type=MESH
        )
        copy.start()
        sends.append(copy)

    def landed(target, send, recv, peer):
        pltpu.make_async_remote_copy(
            src_ref=target, dst_ref=target, send_sem=send, recv_sem=recv, device_id=peer, device_id_type=MESH
        ).wait_recv()

    local = []
    for q in range(3):
        copy = pltpu.make_async_copy(mine(q), whole(q, me), here_sem.at[q])
        copy.start()
        local.append(copy)
        for k in range(1, 4):
            push(mine(q), whole(q, me), z_send.at[q, k], z_recv.at[q, k], z_peer[k])
        push(mine(q), whole(q, me), x_send.at[q, 0], x_recv.at[q, 0], x_peer)
        push(mine(q), whole(q, me), y_send.at[q, 0], y_recv.at[q, 0], y_peer)
    push(col_ref, col_oth, b_send, b_recv, c_peer)

    def along_column(q):
        for k in range(1, 4):
            block = index_of(column[k], y, x)
            landed(whole(q, block), z_send.at[q, k], z_recv.at[q, k], z_peer[k])
            push(whole(q, block), whole(q, block), x_send.at[q, k], x_recv.at[q, k], x_peer)
            push(whole(q, block), whole(q, block), y_send.at[q, k], y_recv.at[q, k], y_peer)

    def round_corner(q):
        for k in range(4):
            beside = index_of(column[k], y, 1 - x)
            landed(whole(q, beside), x_send.at[q, k], x_recv.at[q, k], x_peer)
            push(part(q, beside, 0), part(q, beside, 0), d_send.at[q, k, 0], d_recv.at[q, k, 0], y_peer)
            beside = index_of(column[k], 1 - y, x)
            landed(whole(q, beside), y_send.at[q, k], y_recv.at[q, k], y_peer)
            push(part(q, beside, 1), part(q, beside, 1), d_send.at[q, k, 1], d_recv.at[q, k, 1], x_peer)

    def to_other_core(q):
        local[q].wait()
        for k in range(4):
            across = index_of(column[k], 1 - y, 1 - x)
            landed(part(q, across, 0), d_send.at[q, k, 0], d_recv.at[q, k, 0], y_peer)
            landed(part(q, across, 1), d_send.at[q, k, 1], d_recv.at[q, k, 1], x_peer)
            layer = index_of(column[k], 0, 0)
            push(whole(q, layer, 4), whole(q, layer, 4, True), c_send.at[q, k], c_recv.at[q, k], c_peer)

    along_column(0)
    round_corner(0)
    along_column(1)
    round_corner(1)
    to_other_core(0)
    along_column(2)
    round_corner(2)
    to_other_core(1)
    to_other_core(2)
    for q in range(3):
        for k in range(4):
            layer = index_of(column[k], 0, 0)
            landed(whole(q, layer, 4, True), c_send.at[q, k], c_recv.at[q, k], c_peer)
    landed(col_oth, b_send, b_recv, c_peer)
    for copy in sends:
        copy.wait_send()


def gather_weights(attn_low, ffn_low, col_bias):
    count, rows, width = attn_low.shape
    hidden = ffn_low.shape[2]
    full = rows * 16
    attn_shape = jax.ShapeDtypeStruct((count, full, width), BF16)
    ffn_shape = jax.ShapeDtypeStruct((2, full, hidden), BF16)
    dma = pltpu.SemaphoreType.DMA
    col = col_bias.reshape(-1, LANES)
    anywhere = pl.BlockSpec(memory_space=pltpu.HBM)
    outs = pl.pallas_call(
        gather_kernel,
        out_shape=(attn_shape, ffn_shape, attn_shape, ffn_shape, jax.ShapeDtypeStruct(col.shape, F32)),
        in_specs=[anywhere] * 3,
        out_specs=(anywhere,) * 5,
        scratch_shapes=[
            dma((3, 4)), dma((3, 4)), dma((3, 4)), dma((3, 4)), dma((3, 4)), dma((3, 4)),
            dma((3, 4, 2)), dma((3, 4, 2)), dma((3, 4)), dma((3, 4)), dma(()), dma(()), dma((3,)),
        ],
        compiler_params=pltpu.CompilerParams(collective_id=0, has_side_effects=True),
        name="gather_weights",
    )(attn_low, ffn_low, col)
    attn_own, ffn_own, attn_oth, ffn_oth, col_oth = outs
    return (attn_own, attn_oth), (ffn_own, ffn_oth), (col_bias, col_oth.reshape(-1))


def exchange_kernel(total, mine_ref, all_ref, here_sem, send_sem, recv_sem):
    me = lax.axis_index("dp") * 2 + lax.axis_index("mp")

    def device(step):
        rank = lax.rem(me + step, total)
        return (rank // 2, lax.rem(rank, 2))

    barrier = pltpu.get_barrier_semaphore()
    for step in range(1, total):
        pl.semaphore_signal(barrier, inc=1, device_id=device(step), device_id_type=MESH)
    pl.semaphore_wait(barrier, total - 1)
    local = pltpu.make_async_copy(mine_ref, all_ref.at[me], here_sem)
    local.start()
    copies = []
    for step in range(1, total):
        copy = pltpu.make_async_remote_copy(
            src_ref=mine_ref,
            dst_ref=all_ref.at[me],
            send_sem=send_sem.at[step],
            recv_sem=recv_sem.at[step],
            device_id=device(step),
            device_id_type=MESH,
        )
        copy.start()
        copies.append(copy)
    local.wait()
    for copy in copies:
        copy.wait()


def gather_rows(mine, total):
    slabs = mine.reshape(-1, LANES)
    every = pl.pallas_call(
        functools.partial(exchange_kernel, total),
        out_shape=jax.ShapeDtypeStruct((total,) + slabs.shape, F32),
        in_specs=[pl.BlockSpec(memory_space=pltpu.VMEM)],
        out_specs=pl.BlockSpec(memory_space=pltpu.VMEM),
        scratch_shapes=[
            pltpu.SemaphoreType.DMA(()),
            pltpu.SemaphoreType.DMA((total,)),
            pltpu.SemaphoreType.DMA((total,)),
        ],
        compiler_params=pltpu.CompilerParams(collective_id=1, has_side_effects=True),
        name="gather_rows",
    )(slabs)
    return every.reshape(total, -1)


def first_head(shape):
    return lax.broadcasted_iota(jnp.int32, shape, 1) < HD


def attend_kernel(spans, lens_ref, q_ref, k_ref, v_ref, o_ref):
    for index, (start, slots) in enumerate(spans):
        length = lens_ref[index]
        keys = k_ref[0, pl.ds(start, slots), :]
        values = v_ref[0, pl.ds(start, slots), :]
        lane = first_head(keys.shape)
        scaled = keys * jnp.asarray(HD**-0.5, BF16)
        zero = jnp.zeros_like(scaled)
        head_keys = (jnp.where(lane, scaled, zero), jnp.where(lane, zero, scaled))
        block = min(slots, 256)
        for at in range(0, slots, block):
            queries = q_ref[0, pl.ds(start + at, block), :]
            outs = []
            for head in range(2):
                scores = mm_nt(queries, head_keys[head])
                valid = lax.broadcasted_iota(jnp.int32, scores.shape, 1) < length
                scores = jnp.where(valid, scores, NEG_FILL)
                top = jnp.max(scores, axis=1, keepdims=True)
                weight = jnp.exp(scores - top)
                total = jnp.sum(weight, axis=1, keepdims=True)
                probs = (weight * (1.0 / total)).astype(BF16)
                outs.append(mm(probs, values))
            o_ref[pl.ds(start + at, block), :] = jnp.where(
                first_head(outs[0].shape), outs[0], outs[1]
            ).astype(BF16)


def attend_back_kernel(spans, lens_ref, q_ref, k_ref, v_ref, g_ref, d_ref):
    scale = HD**-0.5
    for index, (start, slots) in enumerate(spans):
        length = lens_ref[index]
        keys = k_ref[0, pl.ds(start, slots), :]
        values = v_ref[0, pl.ds(start, slots), :]
        lane = first_head(keys.shape)
        scaled = keys * jnp.asarray(scale, BF16)
        zero = jnp.zeros_like(scaled)
        head_keys = (jnp.where(lane, scaled, zero), jnp.where(lane, zero, scaled))
        head_values = (jnp.where(lane, values, zero), jnp.where(lane, zero, values))
        block = min(slots, 256)
        grad_k = [None, None]
        grad_v = [None, None]
        for at in range(0, slots, block):
            queries = q_ref[0, pl.ds(start + at, block), :]
            grads = g_ref[pl.ds(start + at, block), :]
            grad_q = []
            for head in range(2):
                scores = mm_nt(head_keys[head], queries)
                valid = lax.broadcasted_iota(jnp.int32, scores.shape, 0) < length
                scores = jnp.where(valid, scores, NEG_FILL)
                top = jnp.max(scores, axis=0, keepdims=True)
                weight = jnp.exp(scores - top)
                total = jnp.sum(weight, axis=0, keepdims=True)
                probs = weight * (1.0 / total)
                grad_probs = mm_nt(head_values[head], grads)
                inner = jnp.sum(probs * grad_probs, axis=0, keepdims=True)
                grad_scores = (probs * (grad_probs - inner)).astype(BF16)
                part_v = mm(probs.astype(BF16), grads)
                part_k = mm(grad_scores, queries)
                grad_v[head] = part_v if at == 0 else grad_v[head] + part_v
                grad_k[head] = part_k if at == 0 else grad_k[head] + part_k
                grad_q.append(mm_tn(grad_scores, keys))
            d_ref[0, pl.ds(start + at, block), :] = (
                jnp.where(first_head(grad_q[0].shape), grad_q[0], grad_q[1]) * scale
            ).astype(BF16)
        d_ref[1, pl.ds(start, slots), :] = (jnp.where(lane, grad_k[0], grad_k[1]) * scale).astype(BF16)
        d_ref[2, pl.ds(start, slots), :] = jnp.where(lane, grad_v[0], grad_v[1]).astype(BF16)


def head_specs(tokens):
    return [pl.BlockSpec((1, tokens, LANES), functools.partial(lambda s, i, lens: (s, 0, i), s)) for s in range(3)]


def attend(proj, lens, spans):
    _, tokens, width = proj.shape
    flops = sum(4 * slots * slots * width for _, slots in spans)
    return pl.pallas_call(
        functools.partial(attend_kernel, spans),
        out_shape=jax.ShapeDtypeStruct((tokens, width), BF16),
        grid_spec=pltpu.PrefetchScalarGridSpec(
            num_scalar_prefetch=1,
            grid=(width // LANES,),
            in_specs=head_specs(tokens),
            out_specs=pl.BlockSpec((tokens, LANES), lambda i, lens: (0, i)),
        ),
        compiler_params=pltpu.CompilerParams(vmem_limit_bytes=40 * MIB),
        cost_estimate=pl.CostEstimate(flops=8 * flops, bytes_accessed=8 * tokens * width, transcendentals=0),
        name="attend",
    )(lens, proj, proj, proj)


def attend_back(proj, grad_out, lens, spans):
    _, tokens, width = proj.shape
    flops = sum(10 * slots * slots * width for _, slots in spans)
    return pl.pallas_call(
        functools.partial(attend_back_kernel, spans),
        out_shape=jax.ShapeDtypeStruct((3, tokens, width), BF16),
        grid_spec=pltpu.PrefetchScalarGridSpec(
            num_scalar_prefetch=1,
            grid=(width // LANES,),
            in_specs=head_specs(tokens) + [pl.BlockSpec((tokens, LANES), lambda i, lens: (0, i))],
            out_specs=pl.BlockSpec((3, tokens, LANES), lambda i, lens: (0, 0, i)),
        ),
        compiler_params=pltpu.CompilerParams(vmem_limit_bytes=40 * MIB),
        cost_estimate=pl.CostEstimate(flops=8 * flops, bytes_accessed=14 * tokens * width, transcendentals=0),
        name="attend_back",
    )(lens, proj, proj, proj, grad_out)


def up_kernel(x_ref, w_ref, b_ref, g_ref, s_ref):
    hidden = mm(x_ref[...], w_ref[0]) + b_ref[...]
    active, slope = gelu_and_slope(hidden)
    g_ref[...] = active.astype(BF16)
    s_ref[...] = slope


def feed_up(low, ffn_half, bias):
    tokens, width = low.shape
    units = ffn_half.shape[2]
    tile = 256
    return pl.pallas_call(
        up_kernel,
        out_shape=(jax.ShapeDtypeStruct((tokens, units), BF16), jax.ShapeDtypeStruct((tokens, units), F32)),
        grid=(units // tile,),
        in_specs=[
            pl.BlockSpec((tokens, width), lambda i: (0, 0)),
            pl.BlockSpec((1, width, tile), lambda i: (0, 0, i)),
            pl.BlockSpec((1, tile), lambda i: (0, i)),
        ],
        out_specs=(pl.BlockSpec((tokens, tile), lambda i: (0, i)), pl.BlockSpec((tokens, tile), lambda i: (0, i))),
        compiler_params=pltpu.CompilerParams(vmem_limit_bytes=40 * MIB),
        cost_estimate=pl.CostEstimate(
            flops=2 * tokens * width * units, bytes_accessed=8 * tokens * units, transcendentals=tokens * units
        ),
        name="feed_up",
    )(low, ffn_half, bias.reshape(1, -1))


def swap_cores(values):
    return lax.ppermute(values, "mp", [(0, 1), (1, 0)])


def scatter_sum(own_parts, other_parts):
    me = lax.axis_index("dp")
    size = lax.axis_size("dp")
    summed = [own + swap_cores(other).astype(F32) for own, other in zip(own_parts, other_parts)]
    if size != 16:
        return [lax.psum_scatter(value, "dp", scatter_dimension=1, tiled=True) for value in summed]
    bits = (lax.rem(me, 2), lax.rem(me // 2, 2))
    level = me // 4
    neighbour = ([(i, i ^ 1) for i in range(16)], [(i, i ^ 2) for i in range(16)])
    columns = []
    for part, value in enumerate(summed):
        count, full, width = value.shape
        value = value.reshape(count, 4, 2, 2, full // 16, width)
        for axis in (0, 1) if part == 0 else (1, 0):
            at = value.ndim - 3 if axis == 0 else 2
            keep = lax.dynamic_index_in_dim(value, bits[axis], at, keepdims=False)
            send = lax.dynamic_index_in_dim(value, 1 - bits[axis], at, keepdims=False).astype(BF16)
            value = keep + lax.ppermute(send, "dp", neighbour[axis]).astype(F32)
        columns.append(value)
    results = []
    for value in columns:
        total = lax.dynamic_index_in_dim(value, level, 1, keepdims=False)
        for step in range(1, 4):
            send = lax.dynamic_index_in_dim(value, lax.rem(level + step, 4), 1, keepdims=False).astype(BF16)
            got = lax.ppermute(send, "dp", [(i, (i + 4 * step) % 16) for i in range(16)])
            total = total + got.astype(F32)
        results.append(total)
    return results


def sum_all(values):
    size = lax.axis_size("dp")
    if size != 16:
        return lax.psum(values, "dp")
    for bit in (1, 2, 4, 8):
        values = values + lax.ppermute(values, "dp", [(i, i ^ bit) for i in range(16)])
    return values


def adam_update(master, first, second, average, grad, rate, decay_w, rates, step_count):
    first_new = rates[0] * first + (1.0 - rates[0]) * grad
    second_new = rates[1] * second + (1.0 - rates[1]) * grad * grad
    fixed_one = first_new / (1.0 - rates[0] ** step_count)
    fixed_two = second_new / (1.0 - rates[1] ** step_count)
    master_new = master - rate * (fixed_one / (jnp.sqrt(fixed_two) + ADAM_EPS) + decay_w * master)
    average_new = rates[2] * average + (1.0 - rates[2]) * master_new
    return (master_new, first_new, second_new, average_new)


def normalize(values):
    center = values - jnp.mean(values, axis=-1, keepdims=True)
    spread = jnp.mean(center * center, axis=-1, keepdims=True)
    inverse = lax.rsqrt(spread + NORM_EPS)
    return center * inverse, inverse


def normalize_back(unit, inverse, grad_unit):
    return inverse * (
        grad_unit
        - jnp.mean(grad_unit, axis=-1, keepdims=True)
        - unit * jnp.mean(grad_unit * unit, axis=-1, keepdims=True)
    )


def per_device(
    query_in,
    passage_in,
    query_len,
    passage_len,
    positive,
    step,
    rates,
    attn_master,
    attn_first,
    attn_second,
    attn_average,
    ffn_master,
    ffn_first,
    ffn_second,
    ffn_average,
    norm_params,
    norm_first,
    norm_second,
    norm_average,
    col_bias,
    col_first,
    col_second,
    col_average,
):
    core = lax.axis_index("mp")
    size = lax.axis_size("dp")
    query_slots, model_width = query_in.shape[1:]
    passage_slots = passage_in.shape[1]
    pairs = query_in.shape[0] * size
    spans = ((0, query_slots), (query_slots, passage_slots))

    def pick(values, index):
        return lax.dynamic_index_in_dim(values, index, 0, keepdims=False)

    tokens = jnp.concatenate([pick(query_in, core), pick(passage_in, core)], axis=0)
    lens = jnp.stack([pick(query_len, core), pick(passage_len, core)])

    attn_low, ffn_low = attn_master.astype(BF16), ffn_master.astype(BF16)
    if size == 16:
        attn_w, ffn_w, col = gather_weights(attn_low, ffn_low, col_bias)
    else:
        attn_full = lax.all_gather(attn_low, "dp", axis=1, tiled=True)
        ffn_full = lax.all_gather(ffn_low, "dp", axis=1, tiled=True)
        attn_w = (attn_full, swap_cores(attn_full))
        ffn_w = (ffn_full, swap_cores(ffn_full))
        col = (col_bias, swap_cores(col_bias))
    width = attn_w[0].shape[2]

    projected, mixed = [], []
    branch = None
    for half in range(2):
        bias = jnp.stack([col[half][:width], jnp.zeros((width,), F32), col[half][width : 2 * width]])
        proj = (
            jnp.einsum("td,sde->ste", tokens, attn_w[half][:3], preferred_element_type=F32) + bias[:, None, :]
        ).astype(BF16)
        out = attend(proj, lens, spans)
        part = mm_nt(out, attn_w[half][3])
        branch = part if branch is None else branch + part
        projected.append(proj)
        mixed.append(out)
    z_one = tokens.astype(F32) + branch + norm_params[0]
    unit_one, inverse_one = normalize(z_one)
    first_norm = unit_one * norm_params[1] + norm_params[2]
    first_low = first_norm.astype(BF16)
    active, slope = [], []
    branch_two = None
    for half in range(2):
        act, slo = feed_up(first_low, ffn_w[half], col[half][2 * width :])
        part = mm_nt(act, ffn_w[half][1])
        branch_two = part if branch_two is None else branch_two + part
        active.append(act)
        slope.append(slo)
    z_two = first_norm + branch_two + norm_params[3]
    unit_two, inverse_two = normalize(z_two)
    places = jnp.arange(query_slots + passage_slots)
    in_query = (places < query_slots) & (places < lens[0])
    in_passage = (places >= query_slots) & (places - query_slots < lens[1])
    share = (
        jnp.stack([in_query, in_passage]).astype(F32) / lens.astype(F32)[:, None]
    )
    mean_unit = jnp.dot(share, unit_two, precision=PRECISE, preferred_element_type=F32)
    pooled = mean_unit * norm_params[4] + norm_params[5]
    shrink = lax.rsqrt(jnp.sum(pooled * pooled, axis=1, keepdims=True) + POOL_EPS)
    embed = pooled * shrink

    target_mine = jnp.broadcast_to(pick(positive, core).astype(F32), (LANES,))
    payload = jnp.concatenate([embed.reshape(-1), target_mine])
    if size == 16:
        every = gather_rows(payload, pairs)
    else:
        every = lax.all_gather(payload, ("dp", "mp"), axis=0)
    every_q = every[:, :model_width]
    every_p = every[:, model_width : 2 * model_width]
    target = (jnp.arange(pairs)[None, :].astype(F32) == every[:, 2 * model_width :][:, :1]).astype(F32)
    logits = lax.dot_general(every_q, every_p, (((1,), (1,)), ((), ())), precision=PRECISE) / SOFTMAX_TEMPER
    row_top = jnp.max(logits, axis=1, keepdims=True)
    exp_logits = jnp.exp(logits - row_top)
    row_total = jnp.sum(exp_logits, axis=1, keepdims=True)
    log_total = row_top[:, 0] + jnp.log(row_total[:, 0])
    loss_value = (jnp.sum(log_total - jnp.sum(logits * target, axis=1)) / pairs).reshape(1)
    grad_logits = (exp_logits / row_total - target) / (pairs * SOFTMAX_TEMPER)
    rank = lax.axis_index("dp") * lax.axis_size("mp") + core
    grad_uq = jnp.dot(pick(grad_logits, rank)[None], every_p, precision=PRECISE)
    grad_up = jnp.dot(
        lax.dynamic_index_in_dim(grad_logits, rank, 1, keepdims=False)[None], every_q, precision=PRECISE
    )
    grad_embed = jnp.concatenate([grad_uq, grad_up], axis=0)

    grad_pooled = shrink * (grad_embed - embed * jnp.sum(grad_embed * embed, axis=1, keepdims=True))
    grad_gain_two = jnp.sum(grad_pooled * mean_unit, axis=0)
    grad_shift_two = jnp.sum(grad_pooled, axis=0)
    grad_unit_two = lax.dot_general(
        share, grad_pooled * norm_params[4], (((0,), (0,)), ((), ())), precision=PRECISE
    )
    grad_ztwo = normalize_back(unit_two, inverse_two, grad_unit_two)
    grad_bias_two = jnp.sum(grad_ztwo, axis=0)
    grad_two_low = grad_ztwo.astype(BF16)

    hidden = ffn_w[0].shape[2]
    cut = hidden // 2

    def two_parts(values):
        return values[:, :cut], values[:, cut:]

    def parted_product(left, halves):
        own = [mm_tn(left, part)[None] for part in two_parts(halves[0])]
        other = [mm_tn(left, part).astype(BF16)[None] for part in two_parts(halves[1])]
        return own, other

    down_grad = scatter_sum(*parted_product(grad_two_low, active))
    grad_hidden, grad_first = [], grad_ztwo
    for half in (1, 0):
        grad_hid = (mm(grad_two_low, ffn_w[half][1]) * slope[half]).astype(BF16)
        grad_hidden.insert(0, grad_hid)
        grad_first = grad_first + mm_nt(grad_hid, ffn_w[half][0])
    grad_hidden_bias = [jnp.sum(value.astype(F32), axis=0) for value in grad_hidden]
    up_grad = scatter_sum(*parted_product(first_low, grad_hidden))

    grad_gain_one = jnp.sum(grad_first * unit_one, axis=0)
    grad_shift_one = jnp.sum(grad_first, axis=0)
    grad_zone = normalize_back(unit_one, inverse_one, grad_first * norm_params[1])
    grad_bias_out = jnp.sum(grad_zone, axis=0)
    grad_one_low = grad_zone.astype(BF16)
    grad_tokens = grad_zone
    grad_query_bias, grad_value_bias, attn_parts = [None, None], [None, None], [None, None]
    for half in (1, 0):
        grad_out = mm(grad_one_low, attn_w[half][3]).astype(BF16)
        grad_proj = attend_back(projected[half], grad_out, lens, spans)
        grad_query_bias[half] = jnp.sum(grad_proj[0].astype(F32), axis=0)
        grad_value_bias[half] = jnp.sum(grad_proj[2].astype(F32), axis=0)
        in_grads = jnp.einsum("td,ste->sde", tokens, grad_proj, preferred_element_type=F32)
        out_grad = mm_tn(grad_one_low, mixed[half])
        parts = [in_grads[:2], jnp.stack([in_grads[2], out_grad])]
        attn_parts[half] = parts if half == 0 else [part.astype(BF16) for part in parts]
        for index in range(3):
            grad_tokens = grad_tokens + mm_nt(grad_proj[index], attn_w[half][index])
    attn_grads = scatter_sum(*attn_parts)

    col_parts = [
        jnp.concatenate([grad_query_bias[half], grad_value_bias[half], grad_hidden_bias[half]]) for half in range(2)
    ]
    norm_part = jnp.stack(
        [grad_bias_out, grad_gain_one, grad_shift_one, grad_bias_two, grad_gain_two, grad_shift_two]
    )
    norm_part = norm_part + swap_cores(norm_part)
    col_part = col_parts[0] + swap_cores(col_parts[1])
    small = sum_all(jnp.concatenate([norm_part.reshape(-1), col_part]))
    norm_grad = small[: norm_part.size].reshape(norm_part.shape)
    col_grad = small[norm_part.size :]

    step_count = step[0].astype(F32)
    attn_grad = jnp.concatenate(attn_grads, axis=0)
    ffn_grad = jnp.stack([jnp.concatenate(parts, axis=-1)[0] for parts in (up_grad, down_grad)])
    attn_out = adam_update(
        attn_master, attn_first, attn_second, attn_average, attn_grad, rates[3], DECAY_WEIGHT, rates, step_count
    )
    ffn_out = adam_update(
        ffn_master, ffn_first, ffn_second, ffn_average, ffn_grad, rates[3], DECAY_WEIGHT, rates, step_count
    )
    norm_out = adam_update(
        norm_params, norm_first, norm_second, norm_average, norm_grad, rates[4], 0.0, rates, step_count
    )
    col_out = adam_update(col_bias, col_first, col_second, col_average, col_grad, rates[4], 0.0, rates, step_count)

    grad_twin = swap_cores(grad_tokens)
    first_pair = jnp.where(core == 0, grad_tokens, grad_twin)
    second_pair = jnp.where(core == 0, grad_twin, grad_tokens)
    query_grad = jnp.stack([first_pair[:query_slots], second_pair[:query_slots]])
    passage_grad = jnp.stack([first_pair[query_slots:], second_pair[query_slots:]])
    return (
        loss_value,
        query_grad,
        passage_grad,
        *attn_out,
        *ffn_out,
        *norm_out,
        *col_out,
        attn_out[0].astype(BF16),
        ffn_out[0].astype(BF16),
    )


def solution(mesh):
    matrix = P(None, "dp", "mp")
    rows = P("dp", None, None)
    placed = (rows, rows, P("dp"), P("dp"), P("dp"), P(), P(), *[matrix] * 8, *[P()] * 4, *[P("mp")] * 4)
    return jax.shard_map(
        per_device,
        mesh=mesh,
        in_specs=placed,
        out_specs=(P(), rows, rows, *[matrix] * 8, *[P()] * 4, *[P("mp")] * 4, matrix, matrix),
        check_vma=False,
    )
```

time: 1060 us -> 381 us (0.36)
  waiting for transfers between devices: 540 us -> 43.6 us
  Pallas kernels: 0 us -> 135 us
  blocking collectives: 124 us -> 0 us
  matrix products: 175 us -> 60.3 us
  local copies, waits for them, and re-layouts: 103 us -> 37.1 us
  starting transfers between devices: 1.01 us -> 45.3 us
  other arithmetic: 82.7 us -> 46.5 us
  between operations: 22.3 us -> 9.24 us
    reduce_scatter x1 -> x0, waiting for transfers between devices: 169 us -> none  [per_device(): lax.psum_scatter(jnp.stack([grad_w_up, grad_w_down]), 'dp', scatter_dimen...]
    unnamed x11 -> x0, waiting for transfers between devices: 166 us -> none
    all_gather x2 -> x0, waiting for transfers between devices: 147 us -> none  [the longest x1 81.2 us: per_device(): lax.all_gather(ffn_master.astype(jnp.bfloat16), 'dp', axis=1, tiled=True)]
    pallas_call x0 -> x8, Pallas kernels: none -> 135 us  [the longest x1 70.7 us: gather_weights(): pl.pallas_call(gather_kernel, out_shape=(attn_shape, ffn_shape, attn_shap...]
    dot_general x35, matrix products: 175 us -> 60.3 us  [the longest x10 23.2 us: mm_tn(): lax.dot_general(left, right, (((0,), (0,)), ((), ())), preferred_element_...]
    psum x1 -> x0, blocking collectives: 80.2 us -> none  [per_device(): loss_value = lax.psum(part_loss.reshape(1), 'dp') / total_pairs]
    psum x4 -> x0, waiting for transfers between devices: 58.3 us -> none  [the longest x1 22.8 us: per_device(): grad_first = lax.psum(first_part, 'mp') + grad_ztwo]
    ppermute x0 -> x43, starting transfers between devices: none -> 45.3 us  [the longest x18 25.2 us: scatter_sum(): lax.ppermute(send, 'dp', [(i, (i + 4 * step) % 16) for i in range(16)])]
  transfers between devices with their start and end apart: 9 -> 43, of which waited for: 8 -> 15; matrix products, arithmetic and copies ran while one was open for 8% -> 19% of each run, Pallas kernels for 0% -> 0%
where the time goes in v1:
time: 381 us; the launch traced here: 377 us
  Pallas kernels  135 us (35%)
  matrix products  60.3 us (16%)
  other arithmetic  46.5 us (12%)
  starting transfers between devices  45.3 us (12%)
  waiting for transfers between devices  43.6 us (11%)
  local copies, waits for them, and re-layouts  37.1 us (10%)
  between operations  9.24 us (2%)
    pallas_call x1, Pallas kernels, gather_weights(): pl.pallas_call(gather_kernel, out_shape=(attn_shape, ffn_shape, attn_shap...  70.7 us
    ppermute x12, waiting for transfers between devices, scatter_sum(): value = keep + lax.ppermute(send, 'dp', neighbour[axis]).astype(F32)  29.9 us
    ppermute x18, starting transfers between devices, scatter_sum(): lax.ppermute(send, 'dp', [(i, (i + 4 * step) % 16) for i in range(16)])  25.2 us
    dot_general x10, matrix products, mm_tn(): lax.dot_general(left, right, (((0,), (0,)), ((), ())), preferred_element_...  23.2 us
    pallas_call x2, Pallas kernels, attend_back(): pl.pallas_call(functools.partial(attend_back_kernel, spans), out_shape=ja...  22.1 us
    pallas_call x2, Pallas kernels, attend(): pl.pallas_call(functools.partial(attend_kernel, spans), out_shape=jax.Sha...  16.8 us
    dot_general x12, matrix products, mm_nt(): lax.dot_general(left, right, (((1,), (1,)), ((), ())), preferred_element_...  15 us
    pallas_call x1, Pallas kernels, gather_rows(): pl.pallas_call(functools.partial(exchange_kernel, total), out_shape=jax.S...  14 us
  transfers between devices with their start and end apart: 43, of which 15 were waited for; matrix products, arithmetic and copies ran while one was open for 19% of the time, Pallas kernels for 0%

profile of v1, /device:TPU:0, one launch (start us, length us, event | category | flops | bytes accessed | tf_op | source)
XLA Modules:
  0.0 377.1 jit_solution(14041908754608307461)
XLA Ops:
  0.7 1.8 convert_element_type.562.attn_ref
  2.5 1.8 convert_element_type.563.ffn_ref
  5.1 70.7 %gather_weights.1 = (bf16[4,768,384]{2,1,0:T(8,128)(2,1)}, bf16[2,768,1536]{2,1,0:T(8,128)(2,1)}, bf16[4,768,384]{2,1,0:T(8,128)(2,1)}, bf16[2,768,1536]{2,1,0:T(8,128)(2,1)}, f32[18,128]{1,0:T(8,128)}) custom-call(bf16[4,48,384]{2,1,0:T(8,128)(2,1)} %convert_element_type.562.attn_ref, bf16[2,48,1536]{2,1,0:T(8,128)(2,1)} %convert_element_type.563.ffn_ref, ...), custom_call_target="tpu_custom_call" | custom-call | tf_op jit(solution)/shard_map/gather_weights/pallas_call | solution.py:178
  80.7 2.8 fusion.29.q_ref.k_ref.v_ref
  83.5 8.5 %attend.2 = bf16[576,384]{1,0:T(8,128)(2,1)S(1)} custom-call(s32[2]{0:T(128)S(1)} %get-tuple-element.81.lens_ref, bf16[3,576,384]{2,1,0:T(8,128)(2,1)S(1)} %fusion.29.q_ref.k_ref.v_ref, bf16[3,576,384]{2,1,0:T(8,128)(2,1)S(1)} %fusion.29.q_ref.k_ref.v_ref, bf16[3,576,384]{2,1,0:T(8,128)(2,1)S(1)} %fusion.29.q_ref.k_ref.v_ref), custom_call_target="tpu_custom_call" | custom-call | flops 3271557120 | bytes 1769472 | tf_op jit(solution)/shard_map/attend/pallas_call | solution.py:321
  92.0 1.9 fusion.76
  95.2 8.3 %attend.3 = bf16[576,384]{1,0:T(8,128)(2,1)S(1)} custom-call(s32[2]{0:T(128)S(1)} %get-tuple-element.81.lens_ref, bf16[3,576,384]{2,1,0:T(8,128)(2,1)S(1)} %fusion.32.q_ref.k_ref.v_ref, bf16[3,576,384]{2,1,0:T(8,128)(2,1)S(1)} %fusion.32.q_ref.k_ref.v_ref, bf16[3,576,384]{2,1,0:T(8,128)(2,1)S(1)} %fusion.32.q_ref.k_ref.v_ref), custom_call_target="tpu_custom_call" | custom-call | flops 3271557120 | bytes 1769472 | tf_op jit(solution)/shard_map/attend/pallas_call | solution.py:321
  105.2 5.7 %feed_up.3 = (bf16[576,1536]{1,0:T(8,128)(2,1)S(1)}, f32[576,1536]{1,0:T(8,128)S(1)}) custom-call(bf16[576,768]{1,0:T(8,128)(2,1)S(1)} %fusion.20.x_ref, bf16[2,768,1536]{2,1,0:T(8,128)(2,1)S(1)} %bitcast.330, f32[1,1536]{1,0:T(1,128)S(1)} %bitcast.337), custom_call_target="tpu_custom_call" | custom-call | flops 1358954496 | bytes 7077888 | tf_op jit(solution)/shard_map/feed_up/pallas_call | solution.py:365
  112.1 1.6 fusion.5
  113.8 5.7 %feed_up.2 = (bf16[576,1536]{1,0:T(8,128)(2,1)S(1)}, f32[576,1536]{1,0:T(8,128)S(1)}) custom-call(bf16[576,768]{1,0:T(8,128)(2,1)S(1)} %fusion.20.x_ref, bf16[2,768,1536]{2,1,0:T(8,128)(2,1)S(1)} %bitcast.334, f32[1,1536]{1,0:T(1,128)S(1)} %reshape.489.b_ref), custom_call_target="tpu_custom_call" | custom-call | flops 1358954496 | bytes 7077888 | tf_op jit(solution)/shard_map/feed_up/pallas_call | solution.py:365
  119.6 1.9 fusion.159
  130.3 14.0 %gather_rows.1 = f32[32,13,128]{2,1,0:T(8,128)} custom-call(f32[13,128]{1,0:T(8,128)} %pad_bitcast_fusion.mine_ref), custom_call_target="tpu_custom_call" | custom-call | tf_op jit(solution)/shard_map/gather_rows/pallas_call | solution.py:226
  156.0 4.0 %fusion.145 = (f32[576]{0:T(1024)S(1)}, f32[576]{0:T(1024)S(1)}, f32[576,768]{1,0:T(8,128)S(1)}) fusion(f32[576]{0:T(1024)} %copy-done.46, f32[576,768]{1,0:T(8,128)} %copy-done.12, f32[576]{0:T(1024)S(1)} %broadcast_multiply_fusion.4, f32[2,768]{1,0:T(2,128)S(1)} %get-tuple-element.75, f32[768]{0:T(1024)S(1)} %get-tuple-element.49, ...), kind=kOutput, calls=%fused_computation.313 | convolution fusion | flops 12832512 | bytes 3558536 | tf_op jit(solution)/shard_map/dot_general | solution.py:563
  164.1 1.6 fusion
  166.8 1.6 convert_reduce_fusion
  168.4 2.1 multiply_reduce_fusion
  174.4 11.0 %attend_back.3 = bf16[3,576,384]{2,1,0:T(8,128)(2,1)S(1)} custom-call(s32[2]{0:T(128)S(1)} %get-tuple-element.81.lens_ref, bf16[3,576,384]{2,1,0:T(8,128)(2,1)S(1)} %copy-done.11, bf16[3,576,384]{2,1,0:T(8,128)(2,1)S(1)} %copy-done.11, bf16[3,576,384]{2,1,0:T(8,128)(2,1)S(1)} %copy-done.11, bf16[576,384]{1,0:T(8,128)(2,1)S(1)} %convolution_convert_fusion.5.g_ref), custom_call_target="tpu_custom_call" | custom-call | flops 8178892800 | bytes 3096576 | tf_op jit(solution)/shard_map/attend_back/pallas_call | solution.py:339
  189.1 11.2 %attend_back.2 = bf16[3,576,384]{2,1,0:T(8,128)(2,1)S(1)} custom-call(s32[2]{0:T(128)S(1)} %get-tuple-element.81.lens_ref, bf16[3,576,384]{2,1,0:T(8,128)(2,1)S(1)} %copy-done.9, bf16[3,576,384]{2,1,0:T(8,128)(2,1)S(1)} %copy-done.9, bf16[3,576,384]{2,1,0:T(8,128)(2,1)S(1)} %copy-done.9, bf16[576,384]{1,0:T(8,128)(2,1)S(1)} %convolution_convert_fusion.6.g_ref), custom_call_target="tpu_custom_call" | custom-call | flops 8178892800 | bytes 3096576 | tf_op jit(solution)/shard_map/attend_back/pallas_call | solution.py:339
  202.2 2.0 add_add_fusion
  205.3 1.6 convert_bitcast_fusion
  209.7 2.2 fusion.38
  212.6 3.3 convolution_bitcast_fusion
  215.9 2.1 fusion.37
  218.1 2.2 fusion.36
  221.9 1.8 collective-permute-start.39
  223.7 3.3 fusion.35
  228.6 1.7 convolution_bitcast_fusion.1
  231.0 1.7 collective-permute-start.41
  234.9 2.1 collective-permute-start.42
  241.2 2.4 slice.306
  244.9 3.1 multiply_add_fusion.7
  248.1 3.1 multiply_add_fusion.5
  251.7 3.6 maximum_add_fusion
  255.3 3.1 copy.80
  258.4 3.7 slice_add_fusion
  262.1 2.2 fusion.57
  265.4 3.8 %bitcast_add_fusion = f32[1,768,768]{2,1,0:T(8,128)} fusion(bf16[1,768,768]{2,1,0:T(8,128)(2,1)} %collective-permute-done.31, bf16[576,768]{1,0:T(8,128)(2,1)S(1)} %copy-done.32, bf16[576,1536]{1,0:T(8,128)(2,1)S(1)} %get-tuple-element.34), kind=kOutput, calls=%fused_computation.9 | convolution fusion | flops 680656896 | bytes 5308416 | tf_op jit(solution)/shard_map/dot_general | solution.py:58
  269.2 3.1 copy.75
  276.0 2.4 bitcast_add_fusion.1
  279.0 2.4 bitcast_add_fusion.2
  281.4 1.6 collective-permute-start.26
  283.0 2.4 bitcast_add_fusion.3
  288.3 6.5 %collective-permute-done.32 = bf16[1,4,2,48,768]{4,3,1,2,0:T(8,128)(2,1)S(1)} collective-permute-done((bf16[1,4,2,48,768]{4,3,1,2,0:T(8,128)(2,1)S(1)}, bf16[1,4,2,48,768]{4,3,1,2,0:T(8,128)(2,1)S(1)}, u32[]{:S(2)}, u32[]{:S(2)}) %collective-permute-start.32) | collective-permute-done | bytes 589856 | tf_op jit(solution)/shard_map/ppermute | solution.py:404
  297.7 2.2 broadcast_select_fusion.1
  300.0 4.0 %collective-permute-done.26 = bf16[1,4,2,48,768]{4,3,1,2,0:T(8,128)(2,1)S(1)} collective-permute-done((bf16[1,4,2,48,768]{4,3,1,2,0:T(8,128)(2,1)S(1)}, bf16[1,4,2,48,768]{4,3,1,2,0:T(8,128)(2,1)S(1)}, u32[]{:S(2)}, u32[]{:S(2)}) %collective-permute-start.26) | collective-permute-done | bytes 589856 | tf_op jit(solution)/shard_map/ppermute | solution.py:404
  305.1 2.4 collective-permute-done.20
  309.0 7.6 %collective-permute-done.14 = bf16[1,4,2,48,768]{4,3,1,2,0:T(8,128)(2,1)S(1)} collective-permute-done((bf16[1,4,2,48,768]{4,3,1,2,0:T(8,128)(2,1)S(1)}, bf16[1,4,2,48,768]{4,3,1,2,0:T(8,128)(2,1)S(1)}, u32[]{:S(2)}, u32[]{:S(2)}) %collective-permute-start.14) | collective-permute-done | bytes 589856 | tf_op jit(solution)/shard_map/ppermute | solution.py:404
  317.7 1.9 pad_maximum_fusion
  319.5 3.4 collective-permute-done.9
  323.8 2.0 collective-permute-start.12
  325.9 3.3 collective-permute-done.33
  330.3 1.6 collective-permute-start.10
  331.9 2.8 collective-permute-done.21
  334.8 1.9 collective-permute-start.6
  336.9 1.6 collective-permute-start.5
  338.7 3.8 %collective-permute-start.36 = (bf16[1,48,768]{2,1,0:T(8,128)(2,1)S(1)}, bf16[1,48,768]{2,1,0:T(8,128)(2,1)S(1)}, u32[]{:S(2)}, u32[]{:S(2)}) collective-permute-start(bf16[1,48,768]{2,1,0:T(8,128)(2,1)S(1)} %get-tuple-element.94), channel_id=1, source_target_pairs={{0,24},{2,26},{4,28},{6,30},{8,0},{10,2},{12,4},{14,6},{16,8},{18,... | collective-permute-start | bytes 221192 | tf_op jit(solution)/shard_map/ppermute | solution.py:411
  344.0 4.3 %collective-permute-done.5 = bf16[2,48,384]{2,1,0:T(8,128)(2,1)S(1)} collective-permute-done((bf16[2,48,384]{2,1,0:T(8,128)(2,1)S(1)}, bf16[2,48,384]{2,1,0:T(8,128)(2,1)S(1)}, u32[]{:S(2)}, u32[]{:S(2)}) %collective-permute-start.5) | collective-permute-done | bytes 73760 | tf_op jit(solution)/shard_map/ppermute | solution.py:411
  348.4 2.8 collective-permute-start.29
  351.2 2.9 fusion.149
  355.6 3.8 %collective-permute-start.24 = (bf16[1,48,768]{2,1,0:T(8,128)(2,1)S(1)}, bf16[1,48,768]{2,1,0:T(8,128)(2,1)S(1)}, u32[]{:S(2)}, u32[]{:S(2)}) collective-permute-start(bf16[1,48,768]{2,1,0:T(8,128)(2,1)S(1)} %get-tuple-element.88), channel_id=1, source_target_pairs={{0,24},{2,26},{4,28},{6,30},{8,0},{10,2},{12,4},{14,6},{16,8},{18,... | collective-permute-start | bytes 221192 | tf_op jit(solution)/shard_map/ppermute | solution.py:411
  360.2 3.2 collective-permute-start.18
  364.7 2.4 collective-permute-done.23
  367.6 1.8 collective-permute-done.17
  370.8 3.5 fusion.147
  (372 shorter events, 81.4 us)
Async XLA Ops:
  0.7 78.4 %copy-start = (bf16[2,512,768]{2,1,0:T(8,128)(2,1)S(1)}, bf16[2,512,768]{2,1,0:T(8,128)(2,1)}, u32[]{:S(2)}) copy-start(bf16[2,512,768]{2,1,0:T(8,128)(2,1)} %param.24) | copy-start | bytes 4718596
  0.7 76.5 %copy-start.41 = (f32[2304]{0:T(1024)S(1)}, f32[2304]{0:T(1024)}, u32[]{:S(2)}) copy-start(f32[2304]{0:T(1024)} %param.42) | copy-start | bytes 27652
  0.7 76.5 %copy-start.44 = (f32[6,768]{1,0:T(8,128)S(1)}, f32[6,768]{1,0:T(8,128)}, u32[]{:S(2)}) copy-start(f32[6,768]{1,0:T(8,128)} %param.38) | copy-start | bytes 55300
  0.7 77.2 %copy-start.74 = (s32[2]{0:T(128)S(1)}, s32[2]{0:T(128)}, u32[]{:S(2)}) copy-start(s32[2]{0:T(128)} %param.26) | copy-start | bytes 28
  0.7 77.7 %copy-start.75 = (s32[2]{0:T(128)S(1)}, s32[2]{0:T(128)}, u32[]{:S(2)}) copy-start(s32[2]{0:T(128)} %param.25) | copy-start | bytes 28
  0.7 78.4 %copy-start.50 = (bf16[2,64,768]{2,1,0:T(8,128)(2,1)S(1)}, bf16[2,64,768]{2,1,0:T(8,128)(2,1)}, u32[]{:S(2)}) copy-start(bf16[2,64,768]{2,1,0:T(8,128)(2,1)} %param.23) | copy-start | bytes 589828
  77.8 26.9 %copy-start.53 = (f32[768]{0:T(1024)}, f32[768]{0:T(1024)S(1)}, u32[]{:S(2)}) copy-start(f32[768]{0:T(1024)S(1)} %get-tuple-element.52) | copy-start | bytes 9220
  77.8 26.9 %copy-start.61 = (f32[768]{0:T(1024)}, f32[768]{0:T(1024)S(1)}, u32[]{:S(2)}) copy-start(f32[768]{0:T(1024)S(1)} %get-tuple-element.51) | copy-start | bytes 9220
  79.1 24.4 %copy-start.20 = (bf16[512,768]{1,0:T(8,128)(2,1)}, bf16[512,768]{1,0:T(8,128)(2,1)S(1)}, u32[]{:S(2)}) copy-start(bf16[512,768]{1,0:T(8,128)(2,1)S(1)} %dynamic-slice_bitcast_fusion) | copy-start | bytes 2359300
  79.1 24.4 %copy-start.36 = (bf16[64,768]{1,0:T(8,128)(2,1)}, bf16[64,768]{1,0:T(8,128)(2,1)S(1)}, u32[]{:S(2)}) copy-start(bf16[64,768]{1,0:T(8,128)(2,1)S(1)} %dynamic-slice_bitcast_fusion.1) | copy-start | bytes 294916
  80.6 42.7 %copy-start.68 = (f32[2]{0:T(128)}, f32[2]{0:T(128)S(1)}, u32[]{:S(2)}) copy-start(f32[2]{0:T(128)S(1)} %get-tuple-element.80) | copy-start | bytes 28
  160.7 55.3 %copy-start.31 = (bf16[576,768]{1,0:T(8,128)(2,1)}, bf16[576,768]{1,0:T(8,128)(2,1)S(1)}, u32[]{:S(2)}) copy-start(bf16[576,768]{1,0:T(8,128)(2,1)S(1)} %convert_element_type.573) | copy-start | bytes 2654212
  172.8 31.5 %copy-start.18 = (bf16[576,768]{1,0:T(8,128)(2,1)}, bf16[576,768]{1,0:T(8,128)(2,1)S(1)}, u32[]{:S(2)}) copy-start(bf16[576,768]{1,0:T(8,128)(2,1)S(1)} %convert_element_type.576) | copy-start | bytes 2654212
  204.2 93.2 %collective-permute-start = (f32[576,768]{1,0:T(8,128)}, f32[576,768]{1,0:T(8,128)}, u32[]{:S(2)}, u32[]{:S(2)}) collective-permute-start(f32[576,768]{1,0:T(8,128)} %add_add_fusion), channel_id=1, source_target_pairs={{0,1},{1,0},{2,3},{3,2},{4,5},{5,4},{6,7},{7,6},{8,9},{9,8},{10,11... | collective-permute-start | bytes 5308424 | tf_op jit(solution)/shard_map/ppermute | solution.py:384
  208.0 43.1 %collective-permute-start.7 = (bf16[2,768,384]{1,2,0:T(8,128)(2,1)}, bf16[2,768,384]{1,2,0:T(8,128)(2,1)}, u32[]{:S(2)}, u32[]{:S(2)}) collective-permute-start(bf16[2,768,384]{1,2,0:T(8,128)(2,1)} %pad_maximum_fusion.1), channel_id=1, source_target_pairs={{0,1},{1,0},{2,3},{3,2},{4,5},{5,4},{6,7},{7,6},{8,9},{9,8},{10,11... | collective-permute-start | bytes 3538952 | tf_op jit(solution)/shard_map/ppermute | solution.py:384
  209.3 49.1 %collective-permute-start.1 = (bf16[2,768,384]{1,2,0:T(8,128)(2,1)}, bf16[2,768,384]{1,2,0:T(8,128)(2,1)}, u32[]{:S(2)}, u32[]{:S(2)}) collective-permute-start(bf16[2,768,384]{1,2,0:T(8,128)(2,1)} %slice.305), channel_id=1, source_target_pairs={{0,1},{1,0},{2,3},{3,2},{4,5},{5,4},{6,7},{7,6},{8,9},{9,8},{10,11... | collective-permute-start | bytes 3538952 | tf_op jit(solution)/shard_map/ppermute | solution.py:384
  211.8 52.4 %collective-permute-start.31 = (bf16[1,768,768]{2,1,0:T(8,128)(2,1)}, bf16[1,768,768]{2,1,0:T(8,128)(2,1)}, u32[]{:S(2)}, u32[]{:S(2)}) collective-permute-start(bf16[1,768,768]{2,1,0:T(8,128)(2,1)} %fusion.38), channel_id=1, source_target_pairs={{0,1},{1,0},{2,3},{3,2},{4,5},{5,4},{6,7},{7,6},{8,9},{9,8},{10,11... | collective-permute-start | bytes 3538952 | tf_op jit(solution)/shard_map/ppermute | solution.py:384
  212.1 8.4 %collective-permute-start.38 = (f32[2304]{0:T(1024)S(1)}, f32[2304]{0:T(1024)S(1)}, u32[]{:S(2)}, u32[]{:S(2)}) collective-permute-start(f32[2304]{0:T(1024)S(1)} %pad_maximum_fusion.6), channel_id=1, source_target_pairs={{0,1},{1,0},{2,3},{3,2},{4,5},{5,4},{6,7},{7,6},{8,9},{9,8},{10,11... | collective-permute-start | bytes 27656 | tf_op jit(solution)/shard_map/ppermute | solution.py:384
  220.6 1.3 collective-permute-start.37
  221.9 5.2 %collective-permute-start.39 = (f32[6912]{0:T(1024)S(1)}, f32[6912]{0:T(1024)S(1)}, u32[]{:S(2)}, u32[]{:S(2)}) collective-permute-start(f32[6912]{0:T(1024)S(1)} %pad_maximum_fusion.5), channel_id=1, source_target_pairs={{0,2},{2,0},{4,6},{6,4},{8,10},{10,8},{12,14},{14,12},{16,18},{18,... | collective-permute-start | bytes 82952 | tf_op jit(solution)/shard_map/ppermute | solution.py:422
  227.1 3.9 %collective-permute-start.40 = (f32[6912]{0:T(1024)S(1)}, f32[6912]{0:T(1024)S(1)}, u32[]{:S(2)}, u32[]{:S(2)}) collective-permute-start(f32[6912]{0:T(1024)S(1)} %fusion.185), channel_id=1, source_target_pairs={{0,4},{2,6},{4,0},{6,2},{8,12},{10,14},{12,8},{14,10},{16,20},{18,... | collective-permute-start | bytes 82952 | tf_op jit(solution)/shard_map/ppermute | solution.py:422
  230.3 17.8 %copy-start.45 = (f32[6,768]{1,0:T(8,128)S(1)}, f32[6,768]{1,0:T(8,128)}, u32[]{:S(2)}) copy-start(f32[6,768]{1,0:T(8,128)} %param.38) | copy-start | bytes 55300
  230.3 17.8 %copy-start.56 = (f32[6,768]{1,0:T(8,128)S(1)}, f32[6,768]{1,0:T(8,128)}, u32[]{:S(2)}) copy-start(f32[6,768]{1,0:T(8,128)} %param.41) | copy-start | bytes 55300
  230.3 17.8 %copy-start.57 = (f32[6,768]{1,0:T(8,128)S(1)}, f32[6,768]{1,0:T(8,128)}, u32[]{:S(2)}) copy-start(f32[6,768]{1,0:T(8,128)} %param.40) | copy-start | bytes 55300
  230.3 17.8 %copy-start.58 = (f32[6,768]{1,0:T(8,128)S(1)}, f32[6,768]{1,0:T(8,128)}, u32[]{:S(2)}) copy-start(f32[6,768]{1,0:T(8,128)} %param.39) | copy-start | bytes 55300
  231.0 3.9 %collective-permute-start.41 = (f32[6912]{0:T(1024)S(1)}, f32[6912]{0:T(1024)S(1)}, u32[]{:S(2)}, u32[]{:S(2)}) collective-permute-start(f32[6912]{0:T(1024)S(1)} %add.545), channel_id=1, source_target_pairs={{0,8},{2,10},{4,12},{6,14},{8,0},{10,2},{12,4},{14,6},{16,24},{18,... | collective-permute-start | bytes 82952 | tf_op jit(solution)/shard_map/ppermute | solution.py:422
  234.9 9.9 %collective-permute-start.42 = (f32[6912]{0:T(1024)S(1)}, f32[6912]{0:T(1024)S(1)}, u32[]{:S(2)}, u32[]{:S(2)}) collective-permute-start(f32[6912]{0:T(1024)S(1)} %add.546), channel_id=1, source_target_pairs={{0,16},{2,18},{4,20},{6,22},{8,24},{10,26},{12,28},{14,30},{16,0},... | collective-permute-start | bytes 82952 | tf_op jit(solution)/shard_map/ppermute | solution.py:422
  244.8 30.3 %collective-permute-start.25 = (bf16[1,768,768]{2,1,0:T(8,128)(2,1)}, bf16[1,768,768]{2,1,0:T(8,128)(2,1)}, u32[]{:S(2)}, u32[]{:S(2)}) collective-permute-start(bf16[1,768,768]{2,1,0:T(8,128)(2,1)} %fusion.37), channel_id=1, source_target_pairs={{0,1},{1,0},{2,3},{3,2},{4,5},{5,4},{6,7},{7,6},{8,9},{9,8},{10,11... | collective-permute-start | bytes 3538952 | tf_op jit(solution)/shard_map/ppermute | solution.py:384
  251.2 27.3 %collective-permute-start.19 = (bf16[1,768,768]{2,1,0:T(8,128)(2,1)}, bf16[1,768,768]{2,1,0:T(8,128)(2,1)}, u32[]{:S(2)}, u32[]{:S(2)}) collective-permute-start(bf16[1,768,768]{2,1,0:T(8,128)(2,1)} %fusion.36), channel_id=1, source_target_pairs={{0,1},{1,0},{2,3},{3,2},{4,5},{5,4},{6,7},{7,6},{8,9},{9,8},{10,11... | collective-permute-start | bytes 3538952 | tf_op jit(solution)/shard_map/ppermute | solution.py:384
  258.4 23.0 %collective-permute-start.13 = (bf16[1,768,768]{2,1,0:T(8,128)(2,1)}, bf16[1,768,768]{2,1,0:T(8,128)(2,1)}, u32[]{:S(2)}, u32[]{:S(2)}) collective-permute-start(bf16[1,768,768]{2,1,0:T(8,128)(2,1)} %fusion.35), channel_id=1, source_target_pairs={{0,1},{1,0},{2,3},{3,2},{4,5},{5,4},{6,7},{7,6},{8,9},{9,8},{10,11... | collective-permute-start | bytes 3538952 | tf_op jit(solution)/shard_map/ppermute | solution.py:384
  264.2 21.4 %collective-permute-start.8 = (bf16[2,4,2,48,384]{4,3,0,1,2:T(8,128)(2,1)}, bf16[2,4,2,48,384]{4,3,0,1,2:T(8,128)(2,1)}, u32[]{:S(2)}, u32[]{:S(2)}) collective-permute-start(bf16[2,4,2,48,384]{4,3,0,1,2:T(8,128)(2,1)} %fusion.57), channel_id=1, source_target_pairs={{0,4},{2,6},{4,0},{6,2},{8,12},{10,14},{12,8},{14,10},{16,20},{18,... | collective-permute-start | bytes 1769480 | tf_op jit(solution)/shard_map/ppermute | solution.py:404
  275.1 21.0 %collective-permute-start.2 = (bf16[2,4,2,48,384]{4,3,2,1,0:T(8,128)(2,1)S(1)}, bf16[2,4,2,48,384]{4,3,2,1,0:T(8,128)(2,1)S(1)}, u32[]{:S(2)}, u32[]{:S(2)}) collective-permute-start(bf16[2,4,2,48,384]{4,3,2,1,0:T(8,128)(2,1)S(1)} %fusion.56), channel_id=1, source_target_pairs={{0,2},{2,0},{4,6},{6,4},{8,10},{10,8},{12,14},{14,12},{16,18},{18,... | collective-permute-start | bytes 1769480 | tf_op jit(solution)/shard_map/ppermute | solution.py:404
  278.5 16.3 %collective-permute-start.32 = (bf16[1,4,2,48,768]{4,3,1,2,0:T(8,128)(2,1)S(1)}, bf16[1,4,2,48,768]{4,3,1,2,0:T(8,128)(2,1)S(1)}, u32[]{:S(2)}, u32[]{:S(2)}) collective-permute-start(bf16[1,4,2,48,768]{4,3,1,2,0:T(8,128)(2,1)S(1)} %fusion.61), channel_id=1, source_target_pairs={{0,4},{2,6},{4,0},{6,2},{8,12},{10,14},{12,8},{14,10},{16,20},{18,... | collective-permute-start | bytes 1769480 | tf_op jit(solution)/shard_map/ppermute | solution.py:404
  281.4 22.5 %collective-permute-start.26 = (bf16[1,4,2,48,768]{4,3,1,2,0:T(8,128)(2,1)S(1)}, bf16[1,4,2,48,768]{4,3,1,2,0:T(8,128)(2,1)S(1)}, u32[]{:S(2)}, u32[]{:S(2)}) collective-permute-start(bf16[1,4,2,48,768]{4,3,1,2,0:T(8,128)(2,1)S(1)} %fusion.60), channel_id=1, source_target_pairs={{0,2},{2,0},{4,6},{6,4},{8,10},{10,8},{12,14},{14,12},{16,18},{18,... | collective-permute-start | bytes 1769480 | tf_op jit(solution)/shard_map/ppermute | solution.py:404
  285.6 21.8 %collective-permute-start.20 = (bf16[1,4,2,48,768]{4,3,1,2,0:T(8,128)(2,1)S(1)}, bf16[1,4,2,48,768]{4,3,1,2,0:T(8,128)(2,1)S(1)}, u32[]{:S(2)}, u32[]{:S(2)}) collective-permute-start(bf16[1,4,2,48,768]{4,3,1,2,0:T(8,128)(2,1)S(1)} %fusion.59), channel_id=1, source_target_pairs={{0,4},{2,6},{4,0},{6,2},{8,12},{10,14},{12,8},{14,10},{16,20},{18,... | collective-permute-start | bytes 1769480 | tf_op jit(solution)/shard_map/ppermute | solution.py:404
  294.8 21.8 %collective-permute-start.14 = (bf16[1,4,2,48,768]{4,3,1,2,0:T(8,128)(2,1)S(1)}, bf16[1,4,2,48,768]{4,3,1,2,0:T(8,128)(2,1)S(1)}, u32[]{:S(2)}, u32[]{:S(2)}) collective-permute-start(bf16[1,4,2,48,768]{4,3,1,2,0:T(8,128)(2,1)S(1)} %fusion.58), channel_id=1, source_target_pairs={{0,2},{2,0},{4,6},{6,4},{8,10},{10,8},{12,14},{14,12},{16,18},{18,... | collective-permute-start | bytes 1769480 | tf_op jit(solution)/shard_map/ppermute | solution.py:404
  296.1 26.8 %collective-permute-start.9 = (bf16[2,4,48,384]{3,2,0,1:T(8,128)(2,1)S(1)}, bf16[2,4,48,384]{3,2,0,1:T(8,128)(2,1)S(1)}, u32[]{:S(2)}, u32[]{:S(2)}) collective-permute-start(bf16[2,4,48,384]{3,2,0,1:T(8,128)(2,1)S(1)} %fusion.90), channel_id=1, source_target_pairs={{0,2},{2,0},{4,6},{6,4},{8,10},{10,8},{12,14},{14,12},{16,18},{18,... | collective-permute-start | bytes 884744 | tf_op jit(solution)/shard_map/ppermute | solution.py:404
  297.3 26.5 %collective-permute-start.3 = (bf16[2,4,48,384]{3,2,1,0:T(8,128)(2,1)S(1)}, bf16[2,4,48,384]{3,2,1,0:T(8,128)(2,1)S(1)}, u32[]{:S(2)}, u32[]{:S(2)}) collective-permute-start(bf16[2,4,48,384]{3,2,1,0:T(8,128)(2,1)S(1)} %fusion.89), channel_id=1, source_target_pairs={{0,4},{2,6},{4,0},{6,2},{8,12},{10,14},{12,8},{14,10},{16,20},{18,... | collective-permute-start | bytes 884744 | tf_op jit(solution)/shard_map/ppermute | solution.py:404
  303.9 25.3 %collective-permute-start.33 = (bf16[1,4,48,768]{3,2,1,0:T(8,128)(2,1)S(1)}, bf16[1,4,48,768]{3,2,1,0:T(8,128)(2,1)S(1)}, u32[]{:S(2)}, u32[]{:S(2)}) collective-permute-start(bf16[1,4,48,768]{3,2,1,0:T(8,128)(2,1)S(1)} %fusion.94), channel_id=1, source_target_pairs={{0,2},{2,0},{4,6},{6,4},{8,10},{10,8},{12,14},{14,12},{16,18},{18,... | collective-permute-start | bytes 884744 | tf_op jit(solution)/shard_map/ppermute | solution.py:404
  307.5 22.9 %collective-permute-start.27 = (bf16[1,4,48,768]{3,2,1,0:T(8,128)(2,1)S(1)}, bf16[1,4,48,768]{3,2,1,0:T(8,128)(2,1)S(1)}, u32[]{:S(2)}, u32[]{:S(2)}) collective-permute-start(bf16[1,4,48,768]{3,2,1,0:T(8,128)(2,1)S(1)} %fusion.93), channel_id=1, source_target_pairs={{0,4},{2,6},{4,0},{6,2},{8,12},{10,14},{12,8},{14,10},{16,20},{18,... | collective-permute-start | bytes 884744 | tf_op jit(solution)/shard_map/ppermute | solution.py:404
  316.6 18.2 %collective-permute-start.21 = (bf16[1,4,48,768]{3,2,1,0:T(8,128)(2,1)S(1)}, bf16[1,4,48,768]{3,2,1,0:T(8,128)(2,1)S(1)}, u32[]{:S(2)}, u32[]{:S(2)}) collective-permute-start(bf16[1,4,48,768]{3,2,1,0:T(8,128)(2,1)S(1)} %fusion.92), channel_id=1, source_target_pairs={{0,2},{2,0},{4,6},{6,4},{8,10},{10,8},{12,14},{14,12},{16,18},{18,... | collective-permute-start | bytes 884744 | tf_op jit(solution)/shard_map/ppermute | solution.py:404
  322.9 14.0 %collective-permute-start.15 = (bf16[1,4,48,768]{3,2,1,0:T(8,128)(2,1)S(1)}, bf16[1,4,48,768]{3,2,1,0:T(8,128)(2,1)S(1)}, u32[]{:S(2)}, u32[]{:S(2)}) collective-permute-start(bf16[1,4,48,768]{3,2,1,0:T(8,128)(2,1)S(1)} %fusion.91), channel_id=1, source_target_pairs={{0,4},{2,6},{4,0},{6,2},{8,12},{10,14},{12,8},{14,10},{16,20},{18,... | collective-permute-start | bytes 884744 | tf_op jit(solution)/shard_map/ppermute | solution.py:404
  323.8 14.8 %collective-permute-start.12 = (bf16[2,48,384]{2,1,0:T(8,128)(2,1)S(1)}, bf16[2,48,384]{2,1,0:T(8,128)(2,1)S(1)}, u32[]{:S(2)}, u32[]{:S(2)}) collective-permute-start(bf16[2,48,384]{2,1,0:T(8,128)(2,1)S(1)} %get-tuple-element.100), channel_id=1, source_target_pairs={{0,24},{2,26},{4,28},{6,30},{8,0},{10,2},{12,4},{14,6},{16,8},{18,... | collective-permute-start | bytes 221192 | tf_op jit(solution)/shard_map/ppermute | solution.py:411
  329.2 9.5 %collective-permute-start.11 = (bf16[2,48,384]{2,1,0:T(8,128)(2,1)S(1)}, bf16[2,48,384]{2,1,0:T(8,128)(2,1)S(1)}, u32[]{:S(2)}, u32[]{:S(2)}) collective-permute-start(bf16[2,48,384]{2,1,0:T(8,128)(2,1)S(1)} %get-tuple-element.101), channel_id=1, source_target_pairs={{0,16},{2,18},{4,20},{6,22},{8,24},{10,26},{12,28},{14,30},{16,0},... | collective-permute-start | bytes 221192 | tf_op jit(solution)/shard_map/ppermute | solution.py:411
  330.3 12.2 %collective-permute-start.10 = (bf16[2,48,384]{2,1,0:T(8,128)(2,1)S(1)}, bf16[2,48,384]{2,1,0:T(8,128)(2,1)S(1)}, u32[]{:S(2)}, u32[]{:S(2)}) collective-permute-start(bf16[2,48,384]{2,1,0:T(8,128)(2,1)S(1)} %get-tuple-element.99), channel_id=1, source_target_pairs={{0,8},{2,10},{4,12},{6,14},{8,16},{10,18},{12,20},{14,22},{16,24},... | collective-permute-start | bytes 221192 | tf_op jit(solution)/shard_map/ppermute | solution.py:411
  334.8 7.8 %collective-permute-start.6 = (bf16[2,48,384]{2,1,0:T(8,128)(2,1)S(1)}, bf16[2,48,384]{2,1,0:T(8,128)(2,1)S(1)}, u32[]{:S(2)}, u32[]{:S(2)}) collective-permute-start(bf16[2,48,384]{2,1,0:T(8,128)(2,1)S(1)} %get-tuple-element.97), channel_id=1, source_target_pairs={{0,24},{2,26},{4,28},{6,30},{8,0},{10,2},{12,4},{14,6},{16,8},{18,... | collective-permute-start | bytes 221192 | tf_op jit(solution)/shard_map/ppermute | solution.py:411
  336.9 11.4 %collective-permute-start.5 = (bf16[2,48,384]{2,1,0:T(8,128)(2,1)S(1)}, bf16[2,48,384]{2,1,0:T(8,128)(2,1)S(1)}, u32[]{:S(2)}, u32[]{:S(2)}) collective-permute-start(bf16[2,48,384]{2,1,0:T(8,128)(2,1)S(1)} %get-tuple-element.98), channel_id=1, source_target_pairs={{0,16},{2,18},{4,20},{6,22},{8,24},{10,26},{12,28},{14,30},{16,0},... | collective-permute-start | bytes 221192 | tf_op jit(solution)/shard_map/ppermute | solution.py:411
  338.7 9.7 %collective-permute-start.4 = (bf16[2,48,384]{2,1,0:T(8,128)(2,1)S(1)}, bf16[2,48,384]{2,1,0:T(8,128)(2,1)S(1)}, u32[]{:S(2)}, u32[]{:S(2)}) collective-permute-start(bf16[2,48,384]{2,1,0:T(8,128)(2,1)S(1)} %get-tuple-element.96), channel_id=1, source_target_pairs={{0,8},{2,10},{4,12},{6,14},{8,16},{10,18},{12,20},{14,22},{16,24},... | collective-permute-start | bytes 221192 | tf_op jit(solution)/shard_map/ppermute | solution.py:411
  338.7 16.9 %collective-permute-start.36 = (bf16[1,48,768]{2,1,0:T(8,128)(2,1)S(1)}, bf16[1,48,768]{2,1,0:T(8,128)(2,1)S(1)}, u32[]{:S(2)}, u32[]{:S(2)}) collective-permute-start(bf16[1,48,768]{2,1,0:T(8,128)(2,1)S(1)} %get-tuple-element.94), channel_id=1, source_target_pairs={{0,24},{2,26},{4,28},{6,30},{8,0},{10,2},{12,4},{14,6},{16,8},{18,... | collective-permute-start | bytes 221192 | tf_op jit(solution)/shard_map/ppermute | solution.py:411
  342.5 13.1 %collective-permute-start.35 = (bf16[1,48,768]{2,1,0:T(8,128)(2,1)S(1)}, bf16[1,48,768]{2,1,0:T(8,128)(2,1)S(1)}, u32[]{:S(2)}, u32[]{:S(2)}) collective-permute-start(bf16[1,48,768]{2,1,0:T(8,128)(2,1)S(1)} %get-tuple-element.95), channel_id=1, source_target_pairs={{0,16},{2,18},{4,20},{6,22},{8,24},{10,26},{12,28},{14,30},{16,0},... | collective-permute-start | bytes 221192 | tf_op jit(solution)/shard_map/ppermute | solution.py:411
  342.6 16.8 %collective-permute-start.34 = (bf16[1,48,768]{2,1,0:T(8,128)(2,1)S(1)}, bf16[1,48,768]{2,1,0:T(8,128)(2,1)S(1)}, u32[]{:S(2)}, u32[]{:S(2)}) collective-permute-start(bf16[1,48,768]{2,1,0:T(8,128)(2,1)S(1)} %get-tuple-element.93), channel_id=1, source_target_pairs={{0,8},{2,10},{4,12},{6,14},{8,16},{10,18},{12,20},{14,22},{16,24},... | collective-permute-start | bytes 221192 | tf_op jit(solution)/shard_map/ppermute | solution.py:411
  348.4 11.1 %collective-permute-start.30 = (bf16[1,48,768]{2,1,0:T(8,128)(2,1)S(1)}, bf16[1,48,768]{2,1,0:T(8,128)(2,1)S(1)}, u32[]{:S(2)}, u32[]{:S(2)}) collective-permute-start(bf16[1,48,768]{2,1,0:T(8,128)(2,1)S(1)} %get-tuple-element.91), channel_id=1, source_target_pairs={{0,24},{2,26},{4,28},{6,30},{8,0},{10,2},{12,4},{14,6},{16,8},{18,... | collective-permute-start | bytes 221192 | tf_op jit(solution)/shard_map/ppermute | solution.py:411
  348.4 11.8 %collective-permute-start.29 = (bf16[1,48,768]{2,1,0:T(8,128)(2,1)S(1)}, bf16[1,48,768]{2,1,0:T(8,128)(2,1)S(1)}, u32[]{:S(2)}, u32[]{:S(2)}) collective-permute-start(bf16[1,48,768]{2,1,0:T(8,128)(2,1)S(1)} %get-tuple-element.92), channel_id=1, source_target_pairs={{0,16},{2,18},{4,20},{6,22},{8,24},{10,26},{12,28},{14,30},{16,0},... | collective-permute-start | bytes 221192 | tf_op jit(solution)/shard_map/ppermute | solution.py:411
  354.1 20.2 %copy-start.30 = (f32[4,48,384]{2,1,0:T(8,128)}, f32[4,48,384]{2,1,0:T(8,128)S(1)}, u32[]{:S(2)}) copy-start(f32[4,48,384]{2,1,0:T(8,128)S(1)} %get-tuple-element.64) | copy-start | bytes 884740
  354.1 16.6 %copy-start.23 = (f32[2,48,1536]{2,1,0:T(8,128)S(1)}, f32[2,48,1536]{2,1,0:T(8,128)}, u32[]{:S(2)}) copy-start(f32[2,48,1536]{2,1,0:T(8,128)} %param.34) | copy-start | bytes 1769476
  354.1 16.7 %copy-start.33 = (f32[2,48,1536]{2,1,0:T(8,128)S(1)}, f32[2,48,1536]{2,1,0:T(8,128)}, u32[]{:S(2)}) copy-start(f32[2,48,1536]{2,1,0:T(8,128)} %param.36) | copy-start | bytes 1769476
  354.1 16.7 %copy-start.34 = (f32[2,48,1536]{2,1,0:T(8,128)S(1)}, f32[2,48,1536]{2,1,0:T(8,128)}, u32[]{:S(2)}) copy-start(f32[2,48,1536]{2,1,0:T(8,128)} %param.35) | copy-start | bytes 1769476
  355.6 7.8 %collective-permute-start.28 = (bf16[1,48,768]{2,1,0:T(8,128)(2,1)S(1)}, bf16[1,48,768]{2,1,0:T(8,128)(2,1)S(1)}, u32[]{:S(2)}, u32[]{:S(2)}) collective-permute-start(bf16[1,48,768]{2,1,0:T(8,128)(2,1)S(1)} %get-tuple-element.90), channel_id=1, source_target_pairs={{0,8},{2,10},{4,12},{6,14},{8,16},{10,18},{12,20},{14,22},{16,24},... | collective-permute-start | bytes 221192 | tf_op jit(solution)/shard_map/ppermute | solution.py:411
  355.6 8.9 %collective-permute-start.24 = (bf16[1,48,768]{2,1,0:T(8,128)(2,1)S(1)}, bf16[1,48,768]{2,1,0:T(8,128)(2,1)S(1)}, u32[]{:S(2)}, u32[]{:S(2)}) collective-permute-start(bf16[1,48,768]{2,1,0:T(8,128)(2,1)S(1)} %get-tuple-element.88), channel_id=1, source_target_pairs={{0,24},{2,26},{4,28},{6,30},{8,0},{10,2},{12,4},{14,6},{16,8},{18,... | collective-permute-start | bytes 221192 | tf_op jit(solution)/shard_map/ppermute | solution.py:411
  359.4 7.6 %collective-permute-start.23 = (bf16[1,48,768]{2,1,0:T(8,128)(2,1)S(1)}, bf16[1,48,768]{2,1,0:T(8,128)(2,1)S(1)}, u32[]{:S(2)}, u32[]{:S(2)}) collective-permute-start(bf16[1,48,768]{2,1,0:T(8,128)(2,1)S(1)} %get-tuple-element.89), channel_id=1, source_target_pairs={{0,16},{2,18},{4,20},{6,22},{8,24},{10,26},{12,28},{14,30},{16,0},... | collective-permute-start | bytes 221192 | tf_op jit(solution)/shard_map/ppermute | solution.py:411
  359.5 7.5 %collective-permute-start.22 = (bf16[1,48,768]{2,1,0:T(8,128)(2,1)S(1)}, bf16[1,48,768]{2,1,0:T(8,128)(2,1)S(1)}, u32[]{:S(2)}, u32[]{:S(2)}) collective-permute-start(bf16[1,48,768]{2,1,0:T(8,128)(2,1)S(1)} %get-tuple-element.87), channel_id=1, source_target_pairs={{0,8},{2,10},{4,12},{6,14},{8,16},{10,18},{12,20},{14,22},{16,24},... | collective-permute-start | bytes 221192 | tf_op jit(solution)/shard_map/ppermute | solution.py:411
  360.2 7.5 %collective-permute-start.18 = (bf16[1,48,768]{2,1,0:T(8,128)(2,1)S(1)}, bf16[1,48,768]{2,1,0:T(8,128)(2,1)S(1)}, u32[]{:S(2)}, u32[]{:S(2)}) collective-permute-start(bf16[1,48,768]{2,1,0:T(8,128)(2,1)S(1)} %get-tuple-element.85), channel_id=1, source_target_pairs={{0,24},{2,26},{4,28},{6,30},{8,0},{10,2},{12,4},{14,6},{16,8},{18,... | collective-permute-start | bytes 221192 | tf_op jit(solution)/shard_map/ppermute | solution.py:411
  363.4 6.1 %collective-permute-start.17 = (bf16[1,48,768]{2,1,0:T(8,128)(2,1)S(1)}, bf16[1,48,768]{2,1,0:T(8,128)(2,1)S(1)}, u32[]{:S(2)}, u32[]{:S(2)}) collective-permute-start(bf16[1,48,768]{2,1,0:T(8,128)(2,1)S(1)} %get-tuple-element.86), channel_id=1, source_target_pairs={{0,16},{2,18},{4,20},{6,22},{8,24},{10,26},{12,28},{14,30},{16,0},... | collective-permute-start | bytes 221192 | tf_op jit(solution)/shard_map/ppermute | solution.py:411
  364.5 6.2 %collective-permute-start.16 = (bf16[1,48,768]{2,1,0:T(8,128)(2,1)S(1)}, bf16[1,48,768]{2,1,0:T(8,128)(2,1)S(1)}, u32[]{:S(2)}, u32[]{:S(2)}) collective-permute-start(bf16[1,48,768]{2,1,0:T(8,128)(2,1)S(1)} %get-tuple-element.84), channel_id=1, source_target_pairs={{0,8},{2,10},{4,12},{6,14},{8,16},{10,18},{12,20},{14,22},{16,24},... | collective-permute-start | bytes 221192 | tf_op jit(solution)/shard_map/ppermute | solution.py:411
  (67 other events, 386.0 us)
